TPU v7x, 32 devices: a whole 2x2x4 slice. The times are simulated.
32 devices in a mesh: img: 8 (over z, y), gy: 4 (over x, core).
Axes of the slice: x: 2, y: 2, z: 4, core: 2. Of those that a mesh axis runs over, the one named last changes fastest.
Arguments:
- path: float32 [32, 4, 128, 128], P('img', None, 'gy'), may hold values from -1.2 to 1.2
- start_image: float32 [4, 128, 128], P(None, 'gy'), may hold values from -1.2 to 1.2
- end_image: float32 [4, 128, 128], P(None, 'gy'), may hold values from -1.2 to 1.2
- labels: int32 [4, 128, 128], P(None, 'gy'), may hold values from 0 to 3
- mob_table: float32 [4], replicated, may hold values from 0.2 to 2
Outputs:
- new_path: float32 [32, 4, 128, 128], P('img', None, 'gy')
All inputs are finite; a program needn't handle non-finite values.
Results may differ from a plain program's by a relative error of at most 0.0001.
Values sent between devices are 32-bit elements; how exact they have to be, the bound alone decides.
No kernel may reach another device: no remote copies, remote signals or barrier semaphores. Data moves between devices by JAX's collectives and lax.ppermute only.
A program may use at most 64 MiB of HBM per device.

v0:
```python
import jax
import jax.numpy as jnp
from jax import lax
from jax.sharding import PartitionSpec as P

ITERS = 2


time_step = 0.5
stiffness = 0.25
step_length = 0.05


def extended_2(shard, sides, width):
    for axis, dim in sides:
        size, length = (lax.axis_size(axis), shard.shape[dim])
        up = [(i, (i + 1) % size) for i in range(size - 1)]
        down = [(j, i) for i, j in up]
        last = lax.slice_in_dim(shard, length - width, length, axis=dim)
        initial = lax.slice_in_dim(shard, 0, width, axis=dim)
        before = lax.ppermute(last, axis, up)
        after = lax.ppermute(initial, axis, down)
        shard = jnp.concatenate([before, shard, after], axis=dim)
    return shard


def shifted(block, axis, distance):
    devices = range(lax.axis_size(axis))
    route = [(i - distance, i) for i in devices if i - distance in devices]
    return lax.ppermute(block, axis, route)


def mobility(labels, table):
    result = jnp.zeros(labels.shape, jnp.float32)
    for level in range(table.shape[0]):
        result = result + jnp.where(labels == level, table[level], jnp.float32(0.0))
    return result


def laplace(padded):
    centre = padded[..., 1:-1, :]
    total = jnp.roll(centre, 1, -3) + jnp.roll(centre, -1, -3)
    total = total + jnp.roll(centre, 1, -1) + jnp.roll(centre, -1, -1)
    return total + padded[..., 2:, :] + padded[..., :-2, :] - 6.0 * centre


def drift(padded, mob):
    centre = padded[..., 1:-1, :]
    return mob * (stiffness * laplace(padded) + centre - centre * centre * centre)


def per_device(path, start_image, end_image, labels, mob_table):
    count = path.shape[0]
    groups = lax.axis_size("img")
    images = count * groups
    rank = lax.axis_index("img")
    is_first = rank == 0
    is_final = rank == groups - 1
    gy_count = lax.axis_size("gy")
    rows_here = path.shape[2]
    cells = images * path.shape[1] * rows_here * gy_count * path.shape[3]
    mob = mobility(labels, mob_table)
    for step in range(ITERS):
        extended = jnp.concatenate([start_image[None], path], 0)
        padded = extended_2(extended, (("gy", 2),), 1)
        force = drift(padded, mob)
        current = padded[1 : count + 1, :, 1:-1, :]
        start_part = padded[0, :, 1:-1, :]
        ahead = shifted(current[0], "img", -1)
        ahead = jnp.where(is_final, end_image, ahead)
        later = jnp.concatenate([current[1:], ahead[None]], 0)
        wide_res = (later - current) / time_step - force[1:]
        opening = (current[0] - start_part) / time_step - force[0]
        mres = mob * wide_res
        mpad = extended_2(mres, (("gy", 2),), 1)
        previous = shifted(wide_res[-1], "img", 1)
        previous = jnp.where(is_first, opening, previous)
        earlier = jnp.concatenate([previous[None], wide_res[:-1]], 0)
        adjoint = stiffness * laplace(mpad) + (1.0 - 3.0 * path * path) * mres
        grad = (earlier - wide_res) / time_step - adjoint
        flat = grad.reshape(count, groups, -1)
        columns = lax.all_to_all(flat, "img", split_axis=1, concat_axis=0, tiled=True)
        every = columns.shape[0]
        index = jnp.arange(1, every + 1).astype(jnp.float32)[:, None, None]
        scaled = index * columns
        before_g = jnp.cumsum(columns, 0) - columns
        before_q = jnp.cumsum(scaled, 0) - scaled
        coeff = jnp.sum(columns, 0) - jnp.sum(scaled, 0) / (every + 1)
        solved = time_step * time_step * (index * coeff[None] - index * before_g + before_q)
        back = lax.all_to_all(solved, "img", split_axis=0, concat_axis=1, tiled=True)
        update = back.reshape(grad.shape)
        squares = lax.psum(jnp.sum(update * update), ("img", "gy"))
        scale = step_length * lax.rsqrt(squares / cells + 1e-06)
        path = path - scale * update
    return path


def solution(mesh):
    in_specs = (
        P("img", None, "gy", None),
        P(None, "gy", None),
        P(None, "gy", None),
        P(None, "gy", None),
        P(),
    )
    out_specs = P("img", None, "gy", None)
    return jax.shard_map(
        per_device, mesh=mesh, in_specs=in_specs, out_specs=out_specs, check_vma=False
    )
```

profile of v0, /device:TPU:0, one launch (start us, length us, event | category | flops | bytes accessed | tf_op | source)
XLA Modules:
  0.0 188.7 jit_solution(131051156970023099)
XLA Ops:
  0.0 0.9 fusion.70
  0.9 1.3 collective-permute-start
  2.3 3.2 %collective-permute-start.1 = (f32[5,4,1,128]{3,2,1,0:T(1,128)S(1)}, f32[5,4,1,128]{3,2,1,0:T(1,128)S(1)}, u32[]{:S(2)}, u32[]{:S(2)}) collective-permute-start(f32[5,4,1,128]{3,2,1,0:T(1,128)S(1)} %get-tuple-element.32), channel_id=1, source_target_pairs={{0,1},{1,2},{2,3},{4,5},{5,6},{6,7},{8,9},{9,10},{10,11},{12,13},{... | collective-permute-start | bytes 30728 | tf_op jit(solution)/shard_map/ppermute | solution.py:21
  5.4 1.3 collective-permute-start.2
  6.9 0.2 fusion.25
  7.2 0.6 copy-done.7
  7.7 0.6 fusion.84
  8.4 2.5 %select_add_fusion = f32[4,32,128]{2,1,0:T(8,128)S(1)} fusion(s32[4,32,128]{2,1,0:T(8,128)S(1)} %copy-done.6, f32[]{:T(128)} %bitcast.4, f32[]{:T(128)} %bitcast.3, f32[]{:T(128)} %bitcast.2, f32[]{:T(128)} %bitcast.1), kind=kLoop, calls=%fused_computation.139 | loop fusion | flops 180224 | bytes 131088 | tf_op jit(solution)/shard_map/add | solution.py:36
  10.9 0.4 fusion.7
  11.4 1.3 collective-permute-done.2
  13.1 5.3 %collective-permute-start.3 = (f32[4,32,128]{2,1,0:T(8,128)S(1)}, f32[4,32,128]{2,1,0:T(8,128)S(1)}, u32[]{:S(2)}, u32[]{:S(2)}) collective-permute-start(f32[4,32,128]{2,1,0:T(8,128)S(1)} %slice_bitcast_fusion.3), channel_id=1, source_target_pairs={{0,4},{4,8},{8,12},{12,16},{16,20},{20,24},{24,28},{1,5},{5,9},{9,... | collective-permute-start | bytes 196616 | tf_op jit(solution)/shard_map/ppermute | solution.py:30
  18.5 1.3 collective-permute-start.4
  19.8 3.4 %collective-permute-start.5 = (f32[4,4,1,128]{3,2,1,0:T(1,128)S(1)}, f32[4,4,1,128]{3,2,1,0:T(1,128)S(1)}, u32[]{:S(2)}, u32[]{:S(2)}) collective-permute-start(f32[4,4,1,128]{3,2,1,0:T(1,128)S(1)} %get-tuple-element.52), channel_id=1, source_target_pairs={{0,1},{1,2},{2,3},{4,5},{5,6},{6,7},{8,9},{9,10},{10,11},{12,13},{... | collective-permute-start | bytes 24584 | tf_op jit(solution)/shard_map/ppermute | solution.py:21
  23.3 0.8 collective-permute-done.5
  24.0 0.4 fusion.33
  24.5 0.9 copy.6
  25.4 5.7 %all-to-all-start = ((f32[4,8,2048]{2,0,1:T(4,128)}), f32[4,8,2048]{2,0,1:T(4,128)S(1)}, u32[]{:S(2)}, u32[]{:S(2)}) async-start(f32[4,8,2048]{2,0,1:T(4,128)} %copy.6), calls=%async_computation | async-start | bytes 524288 | tf_op jit(solution)/shard_map/all_to_all | solution.py:82
  31.1 9.8 %all-to-all-done = f32[4,8,2048]{2,0,1:T(4,128)S(1)} async-done(((f32[4,8,2048]{2,0,1:T(4,128)}), f32[4,8,2048]{2,0,1:T(4,128)S(1)}, u32[]{:S(2)}, u32[]{:S(2)}) %all-to-all-start) | async-done | bytes 262176 | tf_op jit(solution)/shard_map/all_to_all | solution.py:82
  40.9 0.2 all_to_all.41
  41.1 0.3 fusion.73
  41.4 0.2 fusion.85
  41.7 0.7 add_multiply_fusion.1
  42.4 13.0 %all_to_all.54 = f32[32,1,2048]{2,1,0:T(1,128)S(1)} all-to-all(f32[32,1,2048]{2,1,0:T(1,128)S(1)} %add_multiply_fusion.1), channel_id=1, replica_groups=mesh['img'=8,'gy'=4] {'img'}, dimensions={0} | all-to-all | bytes 524288 | tf_op jit(solution)/shard_map/all_to_all | solution.py:90
  55.4 1.1 multiply_reduce_fusion.1
  56.6 38.9 %psum.14 = f32[]{:T(128)} all-reduce(f32[]{:T(128)} %multiply_reduce_fusion.1), channel_id=1, replica_groups=mesh['img'=8,'gy'=4] {'img','gy'}, use_global_device_ids=true, to_apply=%region_5.6 | all-reduce | flops 1 | bytes 8 | tf_op jit(solution)/shard_map/psum | solution.py:92
  96.5 0.2 fusion.20
  96.6 0.2 fusion.21
  96.9 1.3 collective-permute-start.6
  98.2 3.0 %collective-permute-start.7 = (f32[5,4,1,128]{3,2,1,0:T(1,128)S(1)}, f32[5,4,1,128]{3,2,1,0:T(1,128)S(1)}, u32[]{:S(2)}, u32[]{:S(2)}) collective-permute-start(f32[5,4,1,128]{3,2,1,0:T(1,128)S(1)} %get-tuple-element.22), channel_id=1, source_target_pairs={{0,1},{1,2},{2,3},{4,5},{5,6},{6,7},{8,9},{9,10},{10,11},{12,13},{... | collective-permute-start | bytes 30728 | tf_op jit(solution)/shard_map/ppermute | solution.py:21
  101.2 1.3 collective-permute-start.8
  102.6 0.4 fusion.15
  103.0 5.1 %collective-permute-done.8 = f32[4,32,128]{2,1,0:T(8,128)S(1)} collective-permute-done((f32[4,32,128]{2,1,0:T(8,128)S(1)}, f32[4,32,128]{2,1,0:T(8,128)S(1)}, u32[]{:S(2)}, u32[]{:S(2)}) %collective-permute-start.8) | collective-permute-done | bytes 65568 | tf_op jit(solution)/shard_map/ppermute | solution.py:30
  108.1 1.0 broadcast_multiply_fusion.2
  109.5 4.7 %collective-permute-start.9 = (f32[4,32,128]{2,1,0:T(8,128)S(1)}, f32[4,32,128]{2,1,0:T(8,128)S(1)}, u32[]{:S(2)}, u32[]{:S(2)}) collective-permute-start(f32[4,32,128]{2,1,0:T(8,128)S(1)} %slice_bitcast_fusion), channel_id=1, source_target_pairs={{0,4},{4,8},{8,12},{12,16},{16,20},{20,24},{24,28},{1,5},{5,9},{9,... | collective-permute-start | bytes 196616 | tf_op jit(solution)/shard_map/ppermute | solution.py:30
  114.3 1.3 collective-permute-start.10
  115.6 3.0 %collective-permute-start.11 = (f32[4,4,1,128]{3,2,1,0:T(1,128)S(1)}, f32[4,4,1,128]{3,2,1,0:T(1,128)S(1)}, u32[]{:S(2)}, u32[]{:S(2)}) collective-permute-start(f32[4,4,1,128]{3,2,1,0:T(1,128)S(1)} %get-tuple-element.42), channel_id=1, source_target_pairs={{0,1},{1,2},{2,3},{4,5},{5,6},{6,7},{8,9},{9,10},{10,11},{12,13},{... | collective-permute-start | bytes 24584 | tf_op jit(solution)/shard_map/ppermute | solution.py:21
  118.7 0.8 collective-permute-done.11
  119.4 0.4 fusion.37
  119.9 0.2 copy.8
  120.1 12.8 %all_to_all.55 = f32[4,8,2048]{2,0,1:T(4,128)S(1)} all-to-all(f32[4,8,2048]{2,0,1:T(4,128)S(1)} %copy.8), channel_id=1, replica_groups=mesh['img'=8,'gy'=4] {'img'}, dimensions={1} | all-to-all | bytes 524288 | tf_op jit(solution)/shard_map/all_to_all | solution.py:82
  132.9 0.2 all_to_all.46
  133.1 0.3 fusion.72
  133.4 0.2 fusion.86
  133.6 0.7 add_multiply_fusion
  134.3 12.6 %all_to_all.56 = f32[32,1,2048]{2,1,0:T(1,128)S(1)} all-to-all(f32[32,1,2048]{2,1,0:T(1,128)S(1)} %add_multiply_fusion), channel_id=1, replica_groups=mesh['img'=8,'gy'=4] {'img'}, dimensions={0} | all-to-all | bytes 524288 | tf_op jit(solution)/shard_map/all_to_all | solution.py:90
  147.0 1.1 multiply_reduce_fusion
  148.1 38.9 %psum.15 = f32[]{:T(128)} all-reduce(f32[]{:T(128)} %multiply_reduce_fusion), channel_id=1, replica_groups=mesh['img'=8,'gy'=4] {'img','gy'}, use_global_device_ids=true, to_apply=%region_11.12 | all-reduce | flops 1 | bytes 8 | tf_op jit(solution)/shard_map/psum | solution.py:92
  187.9 0.7 sub.179
  (68 shorter events, 1.9 us)
Async XLA Ops:
  0.0 5.4 %copy-start.2 = (f32[4,4,32,128]{3,2,1,0:T(8,128)S(1)}, f32[4,4,32,128]{3,2,1,0:T(8,128)}, u32[]{:S(2)}) copy-start(f32[4,4,32,128]{3,2,1,0:T(8,128)} %param.5) | copy-start | bytes 786436
  0.9 10.0 %collective-permute-start = (f32[5,4,1,128]{3,2,1,0:T(1,128)S(1)}, f32[5,4,1,128]{3,2,1,0:T(1,128)S(1)}, u32[]{:S(2)}, u32[]{:S(2)}) collective-permute-start(f32[5,4,1,128]{3,2,1,0:T(1,128)S(1)} %get-tuple-element.31), channel_id=1, source_target_pairs={{1,0},{2,1},{3,2},{5,4},{6,5},{7,6},{9,8},{10,9},{11,10},{13,12},{... | collective-permute-start | bytes 30728 | tf_op jit(solution)/shard_map/ppermute | solution.py:22
  2.2 4.5 %copy-start.4 = (f32[4,32,128]{2,1,0:T(8,128)S(1)}, f32[4,32,128]{2,1,0:T(8,128)}, u32[]{:S(2)}) copy-start(f32[4,32,128]{2,1,0:T(8,128)} %param.6) | copy-start | bytes 196612
  2.3 8.7 %collective-permute-start.1 = (f32[5,4,1,128]{3,2,1,0:T(1,128)S(1)}, f32[5,4,1,128]{3,2,1,0:T(1,128)S(1)}, u32[]{:S(2)}, u32[]{:S(2)}) collective-permute-start(f32[5,4,1,128]{3,2,1,0:T(1,128)S(1)} %get-tuple-element.32), channel_id=1, source_target_pairs={{0,1},{1,2},{2,3},{4,5},{5,6},{6,7},{8,9},{9,10},{10,11},{12,13},{... | collective-permute-start | bytes 30728 | tf_op jit(solution)/shard_map/ppermute | solution.py:21
  5.4 7.2 %collective-permute-start.2 = (f32[4,32,128]{2,1,0:T(8,128)S(1)}, f32[4,32,128]{2,1,0:T(8,128)S(1)}, u32[]{:S(2)}, u32[]{:S(2)}) collective-permute-start(f32[4,32,128]{2,1,0:T(8,128)S(1)} %slice_bitcast_fusion.5), channel_id=1, source_target_pairs={{4,0},{8,4},{12,8},{16,12},{20,16},{24,20},{28,24},{5,1},{9,5},{13... | collective-permute-start | bytes 196616 | tf_op jit(solution)/shard_map/ppermute | solution.py:30
  7.1 0.7 copy-start.7
  7.1 1.3 copy-start.6
  10.9 1.7 copy-start.5
  10.9 1.7 copy-start.3
  11.3 1.3 slice-start.1
  13.1 10.1 %collective-permute-start.3 = (f32[4,32,128]{2,1,0:T(8,128)S(1)}, f32[4,32,128]{2,1,0:T(8,128)S(1)}, u32[]{:S(2)}, u32[]{:S(2)}) collective-permute-start(f32[4,32,128]{2,1,0:T(8,128)S(1)} %slice_bitcast_fusion.3), channel_id=1, source_target_pairs={{0,4},{4,8},{8,12},{12,16},{16,20},{20,24},{24,28},{1,5},{5,9},{9,... | collective-permute-start | bytes 196616 | tf_op jit(solution)/shard_map/ppermute | solution.py:30
  18.5 4.8 %collective-permute-start.4 = (f32[4,4,1,128]{3,2,1,0:T(1,128)S(1)}, f32[4,4,1,128]{3,2,1,0:T(1,128)S(1)}, u32[]{:S(2)}, u32[]{:S(2)}) collective-permute-start(f32[4,4,1,128]{3,2,1,0:T(1,128)S(1)} %get-tuple-element.51), channel_id=1, source_target_pairs={{1,0},{2,1},{3,2},{5,4},{6,5},{7,6},{9,8},{10,9},{11,10},{13,12},{... | collective-permute-start | bytes 24584 | tf_op jit(solution)/shard_map/ppermute | solution.py:22
  19.8 4.2 %collective-permute-start.5 = (f32[4,4,1,128]{3,2,1,0:T(1,128)S(1)}, f32[4,4,1,128]{3,2,1,0:T(1,128)S(1)}, u32[]{:S(2)}, u32[]{:S(2)}) collective-permute-start(f32[4,4,1,128]{3,2,1,0:T(1,128)S(1)} %get-tuple-element.52), channel_id=1, source_target_pairs={{0,1},{1,2},{2,3},{4,5},{5,6},{6,7},{8,9},{9,10},{10,11},{12,13},{... | collective-permute-start | bytes 24584 | tf_op jit(solution)/shard_map/ppermute | solution.py:21
  25.4 15.6 %all-to-all-start = ((f32[4,8,2048]{2,0,1:T(4,128)}), f32[4,8,2048]{2,0,1:T(4,128)S(1)}, u32[]{:S(2)}, u32[]{:S(2)}) async-start(f32[4,8,2048]{2,0,1:T(4,128)} %copy.6), calls=%async_computation | async-start | bytes 524288 | tf_op jit(solution)/shard_map/all_to_all | solution.py:82
  96.5 6.1 %copy-start = (f32[4,4,32,128]{3,2,1,0:T(8,128)}, f32[4,4,32,128]{3,2,1,0:T(8,128)S(1)}, u32[]{:S(2)}) copy-start(f32[4,4,32,128]{3,2,1,0:T(8,128)S(1)} %sub.164) | copy-start | bytes 786436
  96.9 5.7 %collective-permute-start.6 = (f32[5,4,1,128]{3,2,1,0:T(1,128)S(1)}, f32[5,4,1,128]{3,2,1,0:T(1,128)S(1)}, u32[]{:S(2)}, u32[]{:S(2)}) collective-permute-start(f32[5,4,1,128]{3,2,1,0:T(1,128)S(1)} %get-tuple-element.21), channel_id=1, source_target_pairs={{1,0},{2,1},{3,2},{5,4},{6,5},{7,6},{9,8},{10,9},{11,10},{13,12},{... | collective-permute-start | bytes 30728 | tf_op jit(solution)/shard_map/ppermute | solution.py:22
  98.2 4.4 %collective-permute-start.7 = (f32[5,4,1,128]{3,2,1,0:T(1,128)S(1)}, f32[5,4,1,128]{3,2,1,0:T(1,128)S(1)}, u32[]{:S(2)}, u32[]{:S(2)}) collective-permute-start(f32[5,4,1,128]{3,2,1,0:T(1,128)S(1)} %get-tuple-element.22), channel_id=1, source_target_pairs={{0,1},{1,2},{2,3},{4,5},{5,6},{6,7},{8,9},{9,10},{10,11},{12,13},{... | collective-permute-start | bytes 30728 | tf_op jit(solution)/shard_map/ppermute | solution.py:21
  101.2 6.8 %collective-permute-start.8 = (f32[4,32,128]{2,1,0:T(8,128)S(1)}, f32[4,32,128]{2,1,0:T(8,128)S(1)}, u32[]{:S(2)}, u32[]{:S(2)}) collective-permute-start(f32[4,32,128]{2,1,0:T(8,128)S(1)} %slice_bitcast_fusion.2), channel_id=1, source_target_pairs={{4,0},{8,4},{12,8},{16,12},{20,16},{24,20},{28,24},{5,1},{9,5},{13... | collective-permute-start | bytes 196616 | tf_op jit(solution)/shard_map/ppermute | solution.py:30
  103.0 5.1 %slice-start = ((f32[4,4,32,128]{3,2,1,0:T(8,128)}), f32[3,4,32,128]{3,2,1,0:T(8,128)S(1)}, s32[]{:S(2)}) async-start(f32[4,4,32,128]{3,2,1,0:T(8,128)} %copy-done), calls=%async_computation.4 | async-start | bytes 393216 | tf_op jit(solution)/shard_map/slice | solution.py:71
  109.5 9.2 %copy-start.1 = (f32[4,4,32,128]{3,2,1,0:T(8,128)S(1)}, f32[4,4,32,128]{3,2,1,0:T(8,128)}, u32[]{:S(2)}) copy-start(f32[4,4,32,128]{3,2,1,0:T(8,128)} %copy-done) | copy-start | bytes 786436
  109.5 9.1 %collective-permute-start.9 = (f32[4,32,128]{2,1,0:T(8,128)S(1)}, f32[4,32,128]{2,1,0:T(8,128)S(1)}, u32[]{:S(2)}, u32[]{:S(2)}) collective-permute-start(f32[4,32,128]{2,1,0:T(8,128)S(1)} %slice_bitcast_fusion), channel_id=1, source_target_pairs={{0,4},{4,8},{8,12},{12,16},{16,20},{20,24},{24,28},{1,5},{5,9},{9,... | collective-permute-start | bytes 196616 | tf_op jit(solution)/shard_map/ppermute | solution.py:30
  114.3 4.4 %collective-permute-start.10 = (f32[4,4,1,128]{3,2,1,0:T(1,128)S(1)}, f32[4,4,1,128]{3,2,1,0:T(1,128)S(1)}, u32[]{:S(2)}, u32[]{:S(2)}) collective-permute-start(f32[4,4,1,128]{3,2,1,0:T(1,128)S(1)} %get-tuple-element.41), channel_id=1, source_target_pairs={{1,0},{2,1},{3,2},{5,4},{6,5},{7,6},{9,8},{10,9},{11,10},{13,12},{... | collective-permute-start | bytes 24584 | tf_op jit(solution)/shard_map/ppermute | solution.py:22
  115.6 3.8 %collective-permute-start.11 = (f32[4,4,1,128]{3,2,1,0:T(1,128)S(1)}, f32[4,4,1,128]{3,2,1,0:T(1,128)S(1)}, u32[]{:S(2)}, u32[]{:S(2)}) collective-permute-start(f32[4,4,1,128]{3,2,1,0:T(1,128)S(1)} %get-tuple-element.42), channel_id=1, source_target_pairs={{0,1},{1,2},{2,3},{4,5},{5,6},{6,7},{8,9},{9,10},{10,11},{12,13},{... | collective-permute-start | bytes 24584 | tf_op jit(solution)/shard_map/ppermute | solution.py:21
where the time goes:
time: 190 us; the launch traced here: 189 us
  blocking collectives  116 us (61%)
  starting transfers between devices  36.1 us (19%)
  waiting for transfers between devices  17.7 us (9%)
  other arithmetic  12.6 us (7%)
  local copies, waits for them, and re-layouts  3.91 us (2%)
  between operations  2.03 us (1%)
    psum x2, blocking collectives, per_device(): squares = lax.psum(jnp.sum(update * update), ('img', 'gy'))  77.8 us
    all_to_all x2, blocking collectives, per_device(): lax.all_to_all(solved, 'img', split_axis=0, concat_axis=1, tiled=True)  25.7 us
    all_to_all x1, blocking collectives, per_device(): lax.all_to_all(flat, 'img', split_axis=1, concat_axis=0, tiled=True)  12.8 us
    ppermute x4, starting transfers between devices, extended_2(): before = lax.ppermute(last, axis, up)  12.6 us
    ppermute x4, starting transfers between devices, shifted(): return lax.ppermute(block, axis, route)  12.6 us
    all_to_all x1, waiting for transfers between devices, per_device(): lax.all_to_all(flat, 'img', split_axis=1, concat_axis=0, tiled=True)  9.83 us
    ppermute x4, waiting for transfers between devices, shifted(): return lax.ppermute(block, axis, route)  6.37 us
    all_to_all x1, starting transfers between devices, per_device(): lax.all_to_all(flat, 'img', split_axis=1, concat_axis=0, tiled=True)  5.72 us
  transfers between devices with their start and end apart: 13, of which 5 were waited for; matrix products, arithmetic and copies ran while one was open for 2% of the time, Pallas kernels for 0%

commit v1 on v0

--- a/solution.py
+++ b/solution.py
@@ -1,6 +1,10 @@
+import functools
+
 import jax
 import jax.numpy as jnp
 from jax import lax
+from jax.experimental import pallas as pl
+from jax.experimental.pallas import tpu as pltpu
 from jax.sharding import PartitionSpec as P
 
 ITERS = 2
@@ -49,7 +53,7 @@
     return mob * (stiffness * laplace(padded) + centre - centre * centre * centre)
 
 
-def per_device(path, start_image, end_image, labels, mob_table):
+def general(path, start_image, end_image, labels, mob_table):
     count = path.shape[0]
     groups = lax.axis_size("img")
     images = count * groups
@@ -95,7 +99,322 @@
     return path
 
 
+def walk(mesh):
+    count = mesh.shape["img"]
+    plain = list(range(count))
+    try:
+        line = mesh.devices.reshape(count, -1)[:, 0]
+        place = [tuple(d.coords) for d in line]
+    except Exception:
+        return plain
+
+    def near(a, b):
+        return sum(abs(p - q) for p, q in zip(place[a], place[b])) <= 1
+
+    def grow(order):
+        if len(order) == count:
+            return order
+        for nxt in plain:
+            if nxt not in order and near(order[-1], nxt):
+                found = grow(order + [nxt])
+                if found:
+                    return found
+        return None
+
+    return grow([0]) or plain
+
+
+def spread(order, position, flip):
+    return jnp.where(flip == 1, order[len(order) - 1 - position], order[position])
+
+
+def pack_kernel(order, path_ref, start_ref, end_ref, labels_ref, table_ref, out_ref):
+    images, planes, rows, lanes = path_ref.shape
+    groups = len(order)
+    flip = lax.rem(lax.axis_index("gy"), 2)
+    rank = lax.axis_index("img")
+    slab = rank // 2
+    odd = lax.rem(rank, 2) == 1
+    for c in range(groups):
+        dest = spread(order, c, flip)
+        for m in range(images):
+            for h in range(2):
+                row = 4 * c + 2 * h
+                parts = [path_ref[m, x, row : row + 2, :] for x in range(planes)]
+                out_ref[dest, 2 * m + h] = jnp.concatenate(parts, 0)
+        extra = []
+        for h in range(2):
+            row = 4 * c + 2 * h
+
+            def tile(ref):
+                parts = [ref[x, row : row + 2, :] for x in range(planes)]
+                return jnp.concatenate(parts, 0)
+
+            label = tile(labels_ref)
+            mob = jnp.zeros(label.shape, jnp.float32)
+            for level in range(table_ref.shape[0]):
+                mob = mob + jnp.where(label == level, table_ref[level], jnp.float32(0.0))
+            ends = jnp.where(slab == 0, tile(start_ref), tile(end_ref))
+            extra.append(jnp.where(slab >= 2, mob, ends))
+        out_ref[dest, 2 * images] = jnp.where(odd, extra[1], extra[0])
+
+
+def lap(tiles, first, r_is_0):
+    out = []
+    pair = [tiles[h] + tiles[h + 1] for h in range(len(tiles) - 1)]
+    for h in range(1, len(tiles) - 1):
+        v = tiles[h]
+        total = pltpu.roll(v, 2, 0) + pltpu.roll(v, 6, 0)
+        total = total + pltpu.roll(v, 1, 1) + pltpu.roll(v, 127, 1)
+        y = jnp.where(r_is_0, pltpu.roll(pair[h - 1], 7, 0), pltpu.roll(pair[h], 1, 0))
+        out.append(total + y - 6.0 * v)
+    return out
+
+
+def pad_zero(tiles):
+    zero = jnp.zeros_like(tiles[0])
+    return [zero] + list(tiles) + [zero]
+
+
+def residual(now, ahead, mob, r_is_0):
+    bend = lap(pad_zero(now), 0, r_is_0)
+    out = []
+    for v, w, q, m in zip(now, ahead, bend, mob):
+        force = m * (stiffness * q + v - v * v * v)
+        out.append((w - v) * (1.0 / time_step) - force)
+    return out
+
+
+def gradient(now, before, resid, mob, r_is_0):
+    mres = [m * r for m, r in zip(mob, resid)]
+    bend = lap(mres, 0, r_is_0)
+    out = []
+    for n, q in enumerate(bend):
+        v = now[n + 1]
+        adjoint = stiffness * q + (1.0 - 3.0 * v * v) * mres[n + 1]
+        out.append((before[n] - resid[n + 1]) * (1.0 / time_step) - adjoint)
+    return out
+
+
+def row_parity(shape):
+    return lax.rem(lax.broadcasted_iota(jnp.int32, shape, 0), 2) == 0
+
+
+def fetch(refs, group, tile_at):
+    out = []
+    for ref in refs:
+        out += [ref[group, tile_at], ref[group, tile_at + 1]]
+    return out
+
+
+def fetch_extra(refs, slab):
+    last = refs[0].shape[1] - 1
+    out = []
+    for ref in refs:
+        out += [ref[2 * slab, last], ref[2 * slab + 1, last]]
+    return out
+
+
+def first_kernel(own_ref, prev_ref, next_ref, w_ref, part_ref):
+    refs = (prev_ref, own_ref, next_ref)
+    groups, per = own_ref.shape[0], own_ref.shape[1] // 2
+    count = groups * per
+    shape = own_ref.shape[2:]
+    even = row_parity(shape)
+    mob = fetch_extra(refs, 2)
+    start = fetch_extra(refs, 0)
+    now = fetch(refs, 0, 0)
+    r0 = residual(start, now, mob, even)
+    zero = jnp.zeros(shape, jnp.float32)
+    carry = tuple(r0[1:-1]), (zero,) * 4, (zero,) * 4
+
+    def group_step(i, carry, last_group):
+        before, psum, w = carry
+        for m in range(per):
+            now = fetch(refs, i, 2 * m)
+            if m < per - 1:
+                ahead = fetch(refs, i, 2 * m + 2)
+            elif last_group:
+                ahead = fetch_extra(refs, 1)
+            else:
+                ahead = fetch(refs, i + 1, 0)
+            mob_now = fetch_extra(refs, 2)
+            resid = residual(now, ahead, mob_now, even)
+            grad = gradient(now, before, resid, mob_now, even)
+            for t in range(4):
+                w_ref[i * per + m, t] = w[t]
+            psum = tuple(p + g for p, g in zip(psum, grad))
+            w = tuple(a - p for a, p in zip(w, psum))
+            before = tuple(resid[1:-1])
+        return before, psum, w
+
+    carry = lax.fori_loop(
+        0, groups - 1, lambda i, c: group_step(i, c, False), carry
+    )
+    _, _, w = group_step(groups - 1, carry, True)
+    for t in range(4):
+        w_ref[count, t] = w[t]
+    share = [w[t] * (1.0 / (count + 1)) for t in (1, 2)]
+
+    def square_step(i, total):
+        for m in range(per):
+            k = i * per + m
+            at = (k + 1).astype(jnp.float32)
+            for n, t in enumerate((1, 2)):
+                u = time_step * time_step * (w_ref[k, t] - at * share[n])
+                total = total + u * u
+        return total
+
+    total = lax.fori_loop(0, groups, square_step, zero)
+    line = jnp.sum(total, axis=0, keepdims=True)
+    part_ref[...] = jnp.broadcast_to(line, part_ref.shape)
+
+
+def second_kernel(cells, order, own_ref, prev_ref, next_ref, w_ref, parts_ref, out_ref, part_ref):
+    refs = (prev_ref, own_ref, next_ref)
+    groups, per = own_ref.shape[0], own_ref.shape[1] // 2
+    count = groups * per
+    shape = own_ref.shape[2:]
+    even = row_parity(shape)
+    scale = step_length * lax.rsqrt(jnp.sum(parts_ref[...]) / cells + 1e-06)
+    scale = scale * (time_step * time_step)
+    gy, rank = lax.axis_index("gy"), lax.axis_index("img")
+    flip = lax.rem(gy, 2)
+    opens = (gy == 0) & (rank == order[0])
+    final = lax.axis_size("gy") - 1
+    last_rank = order[0] if final % 2 else order[-1]
+    closes = (gy == final) & (rank == last_rank)
+    none = jnp.float32(0.0)
+    scales = [jnp.where(opens, none, scale), scale, scale, jnp.where(closes, none, scale)]
+    share = [w_ref[count, t] * (1.0 / (count + 1)) for t in range(4)]
+
+    def moved(i, m):
+        k = i * per + m
+        at = jnp.asarray(k + 1, jnp.int32).astype(jnp.float32)
+        tiles = fetch(refs, i, 2 * m)[1:-1]
+        return [v - s * (w_ref[k, t] - at * c) for t, (v, s, c) in enumerate(zip(tiles, scales, share))]
+
+    mob = fetch_extra(refs, 2)[1:-1]
+    start = fetch_extra(refs, 0)[1:-1]
+    now = moved(0, 0)
+    r0 = residual(start, now, mob, even)
+    zero = jnp.zeros(shape, jnp.float32)
+    carry = tuple(now), tuple(r0[1:-1]), (zero,) * 2, (zero,) * 2
+
+    def group_step(i, carry, last_group):
+        now, before, psum, w = carry
+        for m in range(per):
+            if m < per - 1:
+                ahead = moved(i, m + 1)
+            elif last_group:
+                ahead = fetch_extra(refs, 1)[1:-1]
+            else:
+                ahead = moved(i + 1, 0)
+            resid = residual(now, ahead, mob, even)
+            grad = gradient(now, before, resid, mob, even)
+            for t in range(2):
+                out_ref[i, 4 * m + t] = now[t + 1]
+                out_ref[i, 4 * m + 2 + t] = w[t]
+            psum = tuple(p + g for p, g in zip(psum, grad))
+            w = tuple(a - p for a, p in zip(w, psum))
+            before = tuple(resid[1:-1])
+            now = tuple(ahead)
+        return now, before, psum, w
+
+    carry = lax.fori_loop(
+        0, groups - 1, lambda i, c: group_step(i, c, False), carry
+    )
+    w = group_step(groups - 1, carry, True)[3]
+    share = [v * (1.0 / (count + 1)) for v in w]
+
+    def square_step(i, total):
+        for m in range(per):
+            at = (i * per + m + 1).astype(jnp.float32)
+            for t in range(2):
+                u = time_step * time_step * (out_ref[i, 4 * m + 2 + t] - at * share[t])
+                out_ref[i, 4 * m + 2 + t] = u
+                total = total + u * u
+        return total
+
+    total = lax.fori_loop(0, groups, square_step, zero)
+    line = jnp.sum(total, axis=0, keepdims=True)
+    part_ref[...] = jnp.broadcast_to(line, part_ref.shape)
+
+
+def unpack_kernel(cells, order, data_ref, parts_ref, out_ref):
+    images, planes, rows, lanes = out_ref.shape
+    groups = len(order)
+    scale = step_length * lax.rsqrt(jnp.sum(parts_ref[...]) / cells + 1e-06)
+    flip = lax.rem(lax.axis_index("gy"), 2)
+    for c in range(groups):
+        src = spread(order, c, flip)
+        for m in range(images):
+            for h in range(2):
+                row = 4 * c + 2 * h
+                v = data_ref[src, 4 * m + h] - scale * data_ref[src, 4 * m + 2 + h]
+                for x in range(planes):
+                    out_ref[m, x, row : row + 2, :] = v[2 * x : 2 * x + 2, :]
+
+
+def call(kernel, outs, smem_at=None, count=0):
+    specs = [pl.BlockSpec(memory_space=pltpu.VMEM) for _ in range(count)]
+    if smem_at is not None:
+        specs[smem_at] = pl.BlockSpec(memory_space=pltpu.SMEM)
+    shapes = [jax.ShapeDtypeStruct(s, jnp.float32) for s in outs]
+    out_specs = [pl.BlockSpec(memory_space=pltpu.VMEM) for _ in outs]
+    if len(outs) == 1:
+        shapes, out_specs = shapes[0], out_specs[0]
+    return pl.pallas_call(kernel, out_shape=shapes, in_specs=specs, out_specs=out_specs)
+
+
+def blocked(order, path, start_image, end_image, labels, mob_table):
+    images, planes, rows, lanes = path.shape
+    groups, slabs = lax.axis_size("img"), lax.axis_size("gy")
+    both = ("img", "gy")
+    every = groups * slabs
+    tile = (2 * planes, lanes)
+    cells = images * groups * planes * rows * slabs * lanes
+    line = []
+    for g in range(slabs):
+        line += [i * slabs + g for i in (order[::-1] if g % 2 else order)]
+    ahead = [(line[n], line[n + 1]) for n in range(every - 1)]
+    back = [(b, a) for a, b in ahead]
+
+    def swap(v, axis):
+        return lax.all_to_all(v, axis, split_axis=0, concat_axis=0, tiled=True)
+
+    packed = call(
+        functools.partial(pack_kernel, order), [(groups, 2 * images + 1) + tile], 4, 5
+    )(path, start_image, end_image, labels, mob_table)
+    own = swap(packed, "img")
+    prev = lax.ppermute(own, both, ahead)
+    after = lax.ppermute(own, both, back)
+    w, part = call(
+        first_kernel, [(images * groups + 1, 4) + tile, (every, lanes)], None, 3
+    )(own, prev, after)
+    parts = swap(part, both)
+    moved, part = call(
+        functools.partial(second_kernel, cells, order),
+        [(groups, 4 * images) + tile, (every, lanes)],
+        None,
+        5,
+    )(own, prev, after, w, parts)
+    parts = swap(part, both)
+    home = swap(moved, "img")
+    return call(functools.partial(unpack_kernel, cells, order), [path.shape], None, 2)(home, parts)
+
+
 def solution(mesh):
+    order = walk(mesh)
+
+    def per_device(path, start_image, end_image, labels, mob_table):
+        images, planes, rows, lanes = path.shape
+        groups = lax.axis_size("img")
+        fits = rows == 4 * groups and planes == 4 and lanes == 128 and groups >= 6
+        if fits and ITERS == 2:
+            return blocked(order, path, start_image, end_image, labels, mob_table)
+        return general(path, start_image, end_image, labels, mob_table)
+
     in_specs = (
         P("img", None, "gy", None),
         P(None, "gy", None),

time: 190 us -> 81.4 us (0.43)
  blocking collectives: 116 us -> 56.9 us
  starting transfers between devices: 36.1 us -> 5.84 us
  other arithmetic: 12.6 us -> 0 us
  waiting for transfers between devices: 17.7 us -> 5.44 us
  Pallas kernels: 0 us -> 11.3 us
  local copies, waits for them, and re-layouts: 3.91 us -> 1.43 us
  between operations: 2.03 us -> 0.03 us
    psum x2 -> x0, blocking collectives: 77.8 us -> none  [per_device(): squares = lax.psum(jnp.sum(update * update), ('img', 'gy'))]
    ppermute x12 -> x2, starting transfers between devices: 30.4 us -> 5.84 us  [the longest x1 4.56 us: blocked(): prev = lax.ppermute(own, both, ahead)]
    all_to_all x3 -> x4, blocking collectives: 38.5 us -> 56.9 us  [swap(): return lax.all_to_all(v, axis, split_axis=0, concat_axis=0, tiled=True)]
    pallas_call x0 -> x4, Pallas kernels: none -> 11.3 us  [the longest x1 3.78 us: blocked(): call(functools.partial(second_kernel, cells, order), [(groups, 4 * images...]
    all_to_all x1 -> x0, waiting for transfers between devices: 9.83 us -> none  [per_device(): lax.all_to_all(flat, 'img', split_axis=1, concat_axis=0, tiled=True)]
    all_to_all x1 -> x0, starting transfers between devices: 5.72 us -> none  [per_device(): lax.all_to_all(flat, 'img', split_axis=1, concat_axis=0, tiled=True)]
    reduce_sum x6 -> x0, other arithmetic: 3.03 us -> none  [the longest x2 2.28 us: per_device(): squares = lax.psum(jnp.sum(update * update), ('img', 'gy'))]
    add x1 -> x0, other arithmetic: 2.47 us -> none  [mobility(): result = result + jnp.where(labels == level, table[level], jnp.float32(0.0))]
  transfers between devices with their start and end apart: 13 -> 2, of which waited for: 5 -> 1; matrix products, arithmetic and copies ran while one was open for 2% -> 0% of each run, Pallas kernels for 0% -> 0%
where the time goes in v1:
time: 81.4 us; the launch traced here: 80.9 us
  blocking collectives  56.9 us (70%)
  Pallas kernels  11.3 us (14%)
  starting transfers between devices  5.84 us (7%)
  waiting for transfers between devices  5.44 us (7%)
  local copies, waits for them, and re-layouts  1.43 us (2%)
    all_to_all x4, blocking collectives, swap(): return lax.all_to_all(v, axis, split_axis=0, concat_axis=0, tiled=True)  56.9 us
    ppermute x1, waiting for transfers between devices, blocked(): after = lax.ppermute(own, both, back)  5.44 us
    ppermute x1, starting transfers between devices, blocked(): prev = lax.ppermute(own, both, ahead)  4.56 us
    pallas_call x1, Pallas kernels, blocked(): call(functools.partial(second_kernel, cells, order), [(groups, 4 * images...  3.78 us
    pallas_call x1, Pallas kernels, blocked(): call(first_kernel, [(images * groups + 1, 4) + tile, (every, lanes)], Non...  3.69 us
    pallas_call x1, Pallas kernels, blocked(): call(functools.partial(unpack_kernel, cells, order), [path.shape], None, 2)  1.99 us
    pallas_call x1, Pallas kernels, blocked(): call(functools.partial(pack_kernel, order), [(groups, 2 * images + 1) + t...  1.85 us
  transfers between devices with their start and end apart: 2, of which 1 were waited for; matrix products, arithmetic and copies ran while one was open for 0% of the time, Pallas kernels for 0%

profile of v1, /device:TPU:0, one launch (start us, length us, event | category | flops | bytes accessed | tf_op | source)
XLA Modules:
  0.0 80.9 jit_solution(18367145513940772198)
XLA Ops:
  0.0 1.8 %shard_map.55 = f32[8,9,8,128]{3,2,1,0:T(8,128)} custom-call(f32[4,4,32,128]{3,2,1,0:T(8,128)} %path_ref.1, f32[4,32,128]{2,1,0:T(8,128)} %start_ref.1, f32[4,32,128]{2,1,0:T(8,128)} %end_ref.1, s32[4,32,128]{2,1,0:T(8,128)} %labels_ref.1, f32[4]{0:T(128)} %table_ref.1), custom_call_target="tpu_custom_call" | custom-call | tf_op jit(solution)/shard_map/pallas_call | solution.py:386
  1.9 17.6 %all_to_all.32.own_ref = f32[8,9,8,128]{3,2,1,0:T(8,128)S(1)} all-to-all(f32[8,9,8,128]{3,2,1,0:T(8,128)} %shard_map.55), channel_id=1, replica_groups=mesh['img'=8,'gy'=4] {'img'}, dimensions={0} | all-to-all | bytes 589824 | tf_op jit(solution)/shard_map/all_to_all | solution.py:384
  19.5 0.0 copy-start
  19.5 1.3 %collective-permute-start.1 = (f32[8,9,8,128]{3,2,1,0:T(8,128)S(1)}, f32[8,9,8,128]{3,2,1,0:T(8,128)S(1)}, u32[]{:S(2)}, u32[]{:S(2)}) collective-permute-start(f32[8,9,8,128]{3,2,1,0:T(8,128)S(1)} %all_to_all.32.own_ref), channel_id=1, source_target_pairs={{4,0},{12,4},{8,12},{16,8},{20,16},{28,20},{24,28},{25,24},{29,25}... | collective-permute-start | bytes 884744 | tf_op jit(solution)/shard_map/ppermute | solution.py:391
  20.8 4.6 %collective-permute-start = (f32[8,9,8,128]{3,2,1,0:T(8,128)S(1)}, f32[8,9,8,128]{3,2,1,0:T(8,128)S(1)}, u32[]{:S(2)}, u32[]{:S(2)}) collective-permute-start(f32[8,9,8,128]{3,2,1,0:T(8,128)S(1)} %all_to_all.32.own_ref), channel_id=1, source_target_pairs={{0,4},{4,12},{12,8},{8,16},{16,20},{20,28},{28,24},{24,25},{25,29}... | collective-permute-start | bytes 884744 | tf_op jit(solution)/shard_map/ppermute | solution.py:390
  25.4 5.4 %collective-permute-done.1.next_ref = f32[8,9,8,128]{3,2,1,0:T(8,128)S(1)} collective-permute-done((f32[8,9,8,128]{3,2,1,0:T(8,128)S(1)}, f32[8,9,8,128]{3,2,1,0:T(8,128)S(1)}, u32[]{:S(2)}, u32[]{:S(2)}) %collective-permute-start.1) | collective-permute-done | bytes 294944 | tf_op jit(solution)/shard_map/ppermute | solution.py:391
  30.8 0.0 copy-start.1
  30.8 0.0 collective-permute-done.prev_ref
  30.8 0.0 copy-done
  30.8 0.7 copy-done.1
  31.5 0.0 copy-start.2
  31.5 0.7 copy-done.2
  32.2 3.7 %shard_map.56 = (f32[33,4,8,128]{3,2,1,0:T(8,128)}, f32[32,128]{1,0:T(8,128)}) custom-call(f32[8,9,8,128]{3,2,1,0:T(8,128)} %copy-done, f32[8,9,8,128]{3,2,1,0:T(8,128)} %copy-done.2, f32[8,9,8,128]{3,2,1,0:T(8,128)} %copy-done.1), custom_call_target="tpu_custom_call" | custom-call | tf_op jit(solution)/shard_map/pallas_call | solution.py:392
  35.9 10.2 %all_to_all.33 = f32[32,1,128]{2,1,0:T(1,128)} all-to-all(f32[32,1,128]{2,1,0:T(1,128)} %bitcast.11), channel_id=1, replica_groups=mesh['img'=8,'gy'=4] {'img','gy'}, dimensions={0} | all-to-all | bytes 32768 | tf_op jit(solution)/shard_map/all_to_all | solution.py:384
  46.1 3.8 %shard_map.57 = (f32[8,16,8,128]{3,2,1,0:T(8,128)}, f32[32,128]{1,0:T(8,128)}) custom-call(f32[8,9,8,128]{3,2,1,0:T(8,128)} %copy-done, f32[8,9,8,128]{3,2,1,0:T(8,128)} %copy-done.2, f32[8,9,8,128]{3,2,1,0:T(8,128)} %copy-done.1, f32[33,4,8,128]{3,2,1,0:T(8,128)} %get-tuple-element.9.w_ref, f32[32,128]{1,0:T(8,128)} %bitcast.8), custom_call_target="tpu_custom_call" | custom-call | tf_op jit(solution)/shard_map/pallas_call | solution.py:396
  49.9 10.2 %all_to_all.34 = f32[32,1,128]{2,1,0:T(1,128)} all-to-all(f32[32,1,128]{2,1,0:T(1,128)} %bitcast.10), channel_id=1, replica_groups=mesh['img'=8,'gy'=4] {'img','gy'}, dimensions={0} | all-to-all | bytes 32768 | tf_op jit(solution)/shard_map/all_to_all | solution.py:384
  60.1 18.8 %all_to_all.35.data_ref = f32[8,16,8,128]{3,2,1,0:T(8,128)} all-to-all(f32[8,16,8,128]{3,2,1,0:T(8,128)} %get-tuple-element.11), channel_id=1, replica_groups=mesh['img'=8,'gy'=4] {'img'}, dimensions={0} | all-to-all | bytes 1048576 | tf_op jit(solution)/shard_map/all_to_all | solution.py:384
  78.9 2.0 %shard_map.58 = f32[4,4,32,128]{3,2,1,0:T(8,128)} custom-call(f32[8,16,8,128]{3,2,1,0:T(8,128)} %all_to_all.35.data_ref, f32[32,128]{1,0:T(8,128)} %bitcast.9), custom_call_target="tpu_custom_call" | custom-call | tf_op jit(solution)/shard_map/pallas_call | solution.py:404
Async XLA Ops:
  19.5 11.3 %copy-start = (f32[8,9,8,128]{3,2,1,0:T(8,128)}, f32[8,9,8,128]{3,2,1,0:T(8,128)S(1)}, u32[]{:S(2)}) copy-start(f32[8,9,8,128]{3,2,1,0:T(8,128)S(1)} %all_to_all.32.own_ref) | copy-start | bytes 884740
  19.5 11.3 %collective-permute-start.1 = (f32[8,9,8,128]{3,2,1,0:T(8,128)S(1)}, f32[8,9,8,128]{3,2,1,0:T(8,128)S(1)}, u32[]{:S(2)}, u32[]{:S(2)}) collective-permute-start(f32[8,9,8,128]{3,2,1,0:T(8,128)S(1)} %all_to_all.32.own_ref), channel_id=1, source_target_pairs={{4,0},{12,4},{8,12},{16,8},{20,16},{28,20},{24,28},{25,24},{29,25}... | collective-permute-start | bytes 884744 | tf_op jit(solution)/shard_map/ppermute | solution.py:391
  20.8 10.0 %collective-permute-start = (f32[8,9,8,128]{3,2,1,0:T(8,128)S(1)}, f32[8,9,8,128]{3,2,1,0:T(8,128)S(1)}, u32[]{:S(2)}, u32[]{:S(2)}) collective-permute-start(f32[8,9,8,128]{3,2,1,0:T(8,128)S(1)} %all_to_all.32.own_ref), channel_id=1, source_target_pairs={{0,4},{4,12},{12,8},{8,16},{16,20},{20,28},{28,24},{24,25},{25,29}... | collective-permute-start | bytes 884744 | tf_op jit(solution)/shard_map/ppermute | solution.py:390
  30.8 0.7 copy-start.1
  31.5 0.7 copy-start.2

commit v2 on v1

--- a/solution.py
+++ b/solution.py
@@ -341,30 +341,45 @@
     part_ref[...] = jnp.broadcast_to(line, part_ref.shape)
 
 
-def unpack_kernel(cells, order, data_ref, parts_ref, out_ref):
+def last_kernel(cells, data_ref, parts_ref, out_ref):
+    groups, per = out_ref.shape[0], out_ref.shape[1] // 2
+    scale = step_length * lax.rsqrt(jnp.sum(parts_ref[...]) / cells + 1e-06)
+    for i in range(groups):
+        for m in range(per):
+            for t in range(2):
+                out_ref[i, 2 * m + t] = data_ref[i, 4 * m + t] - scale * data_ref[i, 4 * m + 2 + t]
+
+
+def unpack_kernel(order, data_ref, out_ref):
     images, planes, rows, lanes = out_ref.shape
     groups = len(order)
-    scale = step_length * lax.rsqrt(jnp.sum(parts_ref[...]) / cells + 1e-06)
     flip = lax.rem(lax.axis_index("gy"), 2)
     for c in range(groups):
         src = spread(order, c, flip)
         for m in range(images):
             for h in range(2):
                 row = 4 * c + 2 * h
-                v = data_ref[src, 4 * m + h] - scale * data_ref[src, 4 * m + 2 + h]
+                v = data_ref[src, 2 * m + h]
                 for x in range(planes):
                     out_ref[m, x, row : row + 2, :] = v[2 * x : 2 * x + 2, :]
 
 
-def call(kernel, outs, smem_at=None, count=0):
-    specs = [pl.BlockSpec(memory_space=pltpu.VMEM) for _ in range(count)]
-    if smem_at is not None:
-        specs[smem_at] = pl.BlockSpec(memory_space=pltpu.SMEM)
+VMEM_LIMIT = 16 * 1024 * 1024
+WHOLE_VMEM = 67043328
+
+
+def call(kernel, outs, count, scalars=0, limit=VMEM_LIMIT):
     shapes = [jax.ShapeDtypeStruct(s, jnp.float32) for s in outs]
-    out_specs = [pl.BlockSpec(memory_space=pltpu.VMEM) for _ in outs]
-    if len(outs) == 1:
-        shapes, out_specs = shapes[0], out_specs[0]
-    return pl.pallas_call(kernel, out_shape=shapes, in_specs=specs, out_specs=out_specs)
+    places = [pl.BlockSpec(memory_space=pltpu.VMEM) for _ in outs]
+    single = len(outs) == 1
+    return pl.pallas_call(
+        kernel,
+        out_shape=shapes[0] if single else shapes,
+        in_specs=[pl.BlockSpec(memory_space=pltpu.VMEM)] * count
+        + [pl.BlockSpec(memory_space=pltpu.SMEM)] * scalars,
+        out_specs=places[0] if single else places,
+        compiler_params=pltpu.CompilerParams(vmem_limit_bytes=limit),
+    )
 
 
 def blocked(order, path, start_image, end_image, labels, mob_table):
@@ -384,24 +399,30 @@
         return lax.all_to_all(v, axis, split_axis=0, concat_axis=0, tiled=True)
 
     packed = call(
-        functools.partial(pack_kernel, order), [(groups, 2 * images + 1) + tile], 4, 5
+        functools.partial(pack_kernel, order),
+        [(groups, 2 * images + 1) + tile],
+        4,
+        scalars=1,
+        limit=WHOLE_VMEM,
     )(path, start_image, end_image, labels, mob_table)
     own = swap(packed, "img")
     prev = lax.ppermute(own, both, ahead)
     after = lax.ppermute(own, both, back)
-    w, part = call(
-        first_kernel, [(images * groups + 1, 4) + tile, (every, lanes)], None, 3
-    )(own, prev, after)
+    w, part = call(first_kernel, [(images * groups + 1, 4) + tile, (every, lanes)], 3)(
+        own, prev, after
+    )
     parts = swap(part, both)
     moved, part = call(
         functools.partial(second_kernel, cells, order),
         [(groups, 4 * images) + tile, (every, lanes)],
-        None,
         5,
     )(own, prev, after, w, parts)
     parts = swap(part, both)
-    home = swap(moved, "img")
-    return call(functools.partial(unpack_kernel, cells, order), [path.shape], None, 2)(home, parts)
+    done = call(functools.partial(last_kernel, cells), [(groups, 2 * images) + tile], 2)(
+        moved, parts
+    )
+    home = swap(done, "img")
+    return call(functools.partial(unpack_kernel, order), [path.shape], 1)(home)
 
 
 def solution(mesh):

time: 81.4 us -> 65.8 us (0.81)
  blocking collectives: 56.9 us -> 47.9 us
  Pallas kernels: 11.3 us -> 6.27 us
  local copies, waits for them, and re-layouts: 1.43 us -> 0 us
    all_to_all x4, blocking collectives: 56.9 us -> 47.9 us  [swap(): return lax.all_to_all(v, axis, split_axis=0, concat_axis=0, tiled=True)]
    pallas_call x2 -> x3, Pallas kernels: 5.67 us -> 2.72 us  [the longest x1 1.76 us: blocked(): call(first_kernel, [(images * groups + 1, 4) + tile, (every, lanes)], 3)]
    pallas_call x1, Pallas kernels: 3.78 us -> 1.69 us  [blocked(): call(functools.partial(second_kernel, cells, order), [(groups, 4 * images...]
    unnamed x6 -> x0, local copies, waits for them, and re-layouts: 1.43 us -> none
where the time goes in v2:
time: 65.8 us; the launch traced here: 65.5 us
  blocking collectives  47.9 us (73%)
  Pallas kernels  6.27 us (10%)
  starting transfers between devices  5.84 us (9%)
  waiting for transfers between devices  5.44 us (8%)
    all_to_all x4, blocking collectives, swap(): return lax.all_to_all(v, axis, split_axis=0, concat_axis=0, tiled=True)  47.9 us
    ppermute x1, waiting for transfers between devices, blocked(): after = lax.ppermute(own, both, back)  5.44 us
    ppermute x1, starting transfers between devices, blocked(): prev = lax.ppermute(own, both, ahead)  4.56 us
    pallas_call x1, Pallas kernels, blocked(): call(functools.partial(pack_kernel, order), [(groups, 2 * images + 1) + t...  1.86 us
    pallas_call x1, Pallas kernels, blocked(): call(first_kernel, [(images * groups + 1, 4) + tile, (every, lanes)], 3)  1.76 us
    pallas_call x1, Pallas kernels, blocked(): call(functools.partial(second_kernel, cells, order), [(groups, 4 * images...  1.69 us
  transfers between devices with their start and end apart: 2, of which 1 were waited for; matrix products, arithmetic and copies ran while one was open for 0% of the time, Pallas kernels for 0%

profile of v2, /device:TPU:0, one launch (start us, length us, event | category | flops | bytes accessed | tf_op | source)
XLA Modules:
  0.0 65.5 jit_solution(18433966653956806229)
XLA Ops:
  0.0 1.9 %shard_map.55 = f32[8,9,8,128]{3,2,1,0:T(8,128)} custom-call(f32[4,4,32,128]{3,2,1,0:T(8,128)} %path_ref.1, f32[4,32,128]{2,1,0:T(8,128)} %start_ref.1, f32[4,32,128]{2,1,0:T(8,128)} %end_ref.1, s32[4,32,128]{2,1,0:T(8,128)} %labels_ref.1, f32[4]{0:T(128)} %table_ref.1), custom_call_target="tpu_custom_call" | custom-call | tf_op jit(solution)/shard_map/pallas_call | solution.py:401
  1.9 17.6 %all_to_all.32.own_ref = f32[8,9,8,128]{3,2,1,0:T(8,128)S(1)} all-to-all(f32[8,9,8,128]{3,2,1,0:T(8,128)} %shard_map.55), channel_id=1, replica_groups=mesh['img'=8,'gy'=4] {'img'}, dimensions={0} | all-to-all | bytes 589824 | tf_op jit(solution)/shard_map/all_to_all | solution.py:399
  19.5 1.3 %collective-permute-start.1 = (f32[8,9,8,128]{3,2,1,0:T(8,128)S(1)}, f32[8,9,8,128]{3,2,1,0:T(8,128)S(1)}, u32[]{:S(2)}, u32[]{:S(2)}) collective-permute-start(f32[8,9,8,128]{3,2,1,0:T(8,128)S(1)} %all_to_all.32.own_ref), channel_id=1, source_target_pairs={{4,0},{12,4},{8,12},{16,8},{20,16},{28,20},{24,28},{25,24},{29,25}... | collective-permute-start | bytes 884744 | tf_op jit(solution)/shard_map/ppermute | solution.py:410
  20.8 4.6 %collective-permute-start = (f32[8,9,8,128]{3,2,1,0:T(8,128)S(1)}, f32[8,9,8,128]{3,2,1,0:T(8,128)S(1)}, u32[]{:S(2)}, u32[]{:S(2)}) collective-permute-start(f32[8,9,8,128]{3,2,1,0:T(8,128)S(1)} %all_to_all.32.own_ref), channel_id=1, source_target_pairs={{0,4},{4,12},{12,8},{8,16},{16,20},{20,28},{28,24},{24,25},{25,29}... | collective-permute-start | bytes 884744 | tf_op jit(solution)/shard_map/ppermute | solution.py:409
  25.4 5.4 %collective-permute-done.1.next_ref = f32[8,9,8,128]{3,2,1,0:T(8,128)S(1)} collective-permute-done((f32[8,9,8,128]{3,2,1,0:T(8,128)S(1)}, f32[8,9,8,128]{3,2,1,0:T(8,128)S(1)}, u32[]{:S(2)}, u32[]{:S(2)}) %collective-permute-start.1) | collective-permute-done | bytes 294944 | tf_op jit(solution)/shard_map/ppermute | solution.py:410
  30.8 0.0 collective-permute-done.prev_ref
  30.8 1.8 %shard_map.56 = (f32[33,4,8,128]{3,2,1,0:T(8,128)S(1)}, f32[32,128]{1,0:T(8,128)S(1)}) custom-call(f32[8,9,8,128]{3,2,1,0:T(8,128)S(1)} %all_to_all.32.own_ref, f32[8,9,8,128]{3,2,1,0:T(8,128)S(1)} %collective-permute-done.prev_ref, f32[8,9,8,128]{3,2,1,0:T(8,128)S(1)} %collective-permute-done.1.next_ref), custom_call_target="tpu_custom_call" | custom-call | tf_op jit(solution)/shard_map/pallas_call | solution.py:411
  32.6 9.8 %all_to_all.33 = f32[32,1,128]{2,1,0:T(1,128)S(1)} all-to-all(f32[32,1,128]{2,1,0:T(1,128)S(1)} %bitcast.11), channel_id=1, replica_groups=mesh['img'=8,'gy'=4] {'img','gy'}, dimensions={0} | all-to-all | bytes 32768 | tf_op jit(solution)/shard_map/all_to_all | solution.py:399
  42.3 1.7 %shard_map.57 = (f32[8,16,8,128]{3,2,1,0:T(8,128)S(1)}, f32[32,128]{1,0:T(8,128)S(1)}) custom-call(f32[8,9,8,128]{3,2,1,0:T(8,128)S(1)} %all_to_all.32.own_ref, f32[8,9,8,128]{3,2,1,0:T(8,128)S(1)} %collective-permute-done.prev_ref, f32[8,9,8,128]{3,2,1,0:T(8,128)S(1)} %collective-permute-done.1.next_ref, f32[33,4,8,128]{3,2,1,0:T(8,128)S(1)} %get-tuple-element.9.w_ref, ...), custom_call_target="tpu_custom_call" | custom-call | tf_op jit(solution)/shard_map/pallas_call | solution.py:415
  44.0 8.9 %all_to_all.34 = f32[32,1,128]{2,1,0:T(1,128)S(1)} all-to-all(f32[32,1,128]{2,1,0:T(1,128)S(1)} %bitcast.10), channel_id=1, replica_groups=mesh['img'=8,'gy'=4] {'img','gy'}, dimensions={0} | all-to-all | bytes 32768 | tf_op jit(solution)/shard_map/all_to_all | solution.py:399
  52.9 0.2 shard_map.58
  53.1 11.6 %all_to_all.35.data_ref = f32[8,8,8,128]{3,2,1,0:T(8,128)S(1)} all-to-all(f32[8,8,8,128]{3,2,1,0:T(8,128)S(1)} %shard_map.58), channel_id=1, replica_groups=mesh['img'=8,'gy'=4] {'img'}, dimensions={0} | all-to-all | bytes 524288 | tf_op jit(solution)/shard_map/all_to_all | solution.py:399
  64.7 0.8 %shard_map.59 = f32[4,4,32,128]{3,2,1,0:T(8,128)} custom-call(f32[8,8,8,128]{3,2,1,0:T(8,128)S(1)} %all_to_all.35.data_ref), custom_call_target="tpu_custom_call" | custom-call | tf_op jit(solution)/shard_map/pallas_call | solution.py:425
Async XLA Ops:
  19.5 11.3 %collective-permute-start.1 = (f32[8,9,8,128]{3,2,1,0:T(8,128)S(1)}, f32[8,9,8,128]{3,2,1,0:T(8,128)S(1)}, u32[]{:S(2)}, u32[]{:S(2)}) collective-permute-start(f32[8,9,8,128]{3,2,1,0:T(8,128)S(1)} %all_to_all.32.own_ref), channel_id=1, source_target_pairs={{4,0},{12,4},{8,12},{16,8},{20,16},{28,20},{24,28},{25,24},{29,25}... | collective-permute-start | bytes 884744 | tf_op jit(solution)/shard_map/ppermute | solution.py:410
  20.8 10.0 %collective-permute-start = (f32[8,9,8,128]{3,2,1,0:T(8,128)S(1)}, f32[8,9,8,128]{3,2,1,0:T(8,128)S(1)}, u32[]{:S(2)}, u32[]{:S(2)}) collective-permute-start(f32[8,9,8,128]{3,2,1,0:T(8,128)S(1)} %all_to_all.32.own_ref), channel_id=1, source_target_pairs={{0,4},{4,12},{12,8},{8,16},{16,20},{20,28},{28,24},{24,25},{25,29}... | collective-permute-start | bytes 884744 | tf_op jit(solution)/shard_map/ppermute | solution.py:409

commit v3 on v2

--- a/solution.py
+++ b/solution.py
@@ -159,15 +159,17 @@
         out_ref[dest, 2 * images] = jnp.where(odd, extra[1], extra[0])
 
 
-def lap(tiles, first, r_is_0):
+def lap(tiles):
+    sublanes, lanes = tiles[0].shape
+    r_is_0 = lax.rem(lax.broadcasted_iota(jnp.int32, tiles[0].shape, 0), 2) == 0
     out = []
     pair = [tiles[h] + tiles[h + 1] for h in range(len(tiles) - 1)]
     for h in range(1, len(tiles) - 1):
         v = tiles[h]
-        total = pltpu.roll(v, 2, 0) + pltpu.roll(v, 6, 0)
-        total = total + pltpu.roll(v, 1, 1) + pltpu.roll(v, 127, 1)
-        y = jnp.where(r_is_0, pltpu.roll(pair[h - 1], 7, 0), pltpu.roll(pair[h], 1, 0))
-        out.append(total + y - 6.0 * v)
+        total = pltpu.roll(v, 2, 0) + pltpu.roll(v, sublanes - 2, 0)
+        total = total + pltpu.roll(v, 1, 1) + pltpu.roll(v, lanes - 1, 1)
+        lower, upper = pltpu.roll(pair[h - 1], sublanes - 1, 0), pltpu.roll(pair[h], 1, 0)
+        out.append(total + jnp.where(r_is_0, lower, upper) - 6.0 * v)
     return out
 
 
@@ -176,28 +178,21 @@
     return [zero] + list(tiles) + [zero]
 
 
-def residual(now, ahead, mob, r_is_0):
-    bend = lap(pad_zero(now), 0, r_is_0)
+def residual(now, ahead, mob):
     out = []
-    for v, w, q, m in zip(now, ahead, bend, mob):
+    for v, w, q, m in zip(now, ahead, lap(pad_zero(now)), mob):
         force = m * (stiffness * q + v - v * v * v)
         out.append((w - v) * (1.0 / time_step) - force)
     return out
 
 
-def gradient(now, before, resid, mob, r_is_0):
-    mres = [m * r for m, r in zip(mob, resid)]
-    bend = lap(mres, 0, r_is_0)
+def gradient(now, before, resid, mres):
     out = []
-    for n, q in enumerate(bend):
+    for n, q in enumerate(lap(mres)):
         v = now[n + 1]
         adjoint = stiffness * q + (1.0 - 3.0 * v * v) * mres[n + 1]
         out.append((before[n] - resid[n + 1]) * (1.0 / time_step) - adjoint)
     return out
-
-
-def row_parity(shape):
-    return lax.rem(lax.broadcasted_iota(jnp.int32, shape, 0), 2) == 0
 
 
 def fetch(refs, group, tile_at):
@@ -215,22 +210,22 @@
     return out
 
 
-def first_kernel(own_ref, prev_ref, next_ref, w_ref, part_ref):
+DEGREE = 5
+
+
+def iterations_kernel(order, own_ref, prev_ref, next_ref, field_ref, part_ref, w_ref, mres_ref):
     refs = (prev_ref, own_ref, next_ref)
     groups, per = own_ref.shape[0], own_ref.shape[1] // 2
     count = groups * per
     shape = own_ref.shape[2:]
-    even = row_parity(shape)
-    mob = fetch_extra(refs, 2)
-    start = fetch_extra(refs, 0)
-    now = fetch(refs, 0, 0)
-    r0 = residual(start, now, mob, even)
     zero = jnp.zeros(shape, jnp.float32)
-    carry = tuple(r0[1:-1]), (zero,) * 4, (zero,) * 4
-
-    def group_step(i, carry, last_group):
+    slope = 1.0 / time_step
+
+    def first_group(i, carry, last_group):
         before, psum, w = carry
+        mob = fetch_extra(refs, 2)
         for m in range(per):
+            k = i * per + m
             now = fetch(refs, i, 2 * m)
             if m < per - 1:
                 ahead = fetch(refs, i, 2 * m + 2)
@@ -238,116 +233,164 @@
                 ahead = fetch_extra(refs, 1)
             else:
                 ahead = fetch(refs, i + 1, 0)
-            mob_now = fetch_extra(refs, 2)
-            resid = residual(now, ahead, mob_now, even)
-            grad = gradient(now, before, resid, mob_now, even)
+            resid = residual(now, ahead, mob)
+            mres = [a * b for a, b in zip(mob, resid)]
+            grad = gradient(now, before, resid, mres)
             for t in range(4):
-                w_ref[i * per + m, t] = w[t]
+                w_ref[k, t] = w[t]
+            for t in range(2):
+                mres_ref[k, t] = mres[t + 2]
             psum = tuple(p + g for p, g in zip(psum, grad))
             w = tuple(a - p for a, p in zip(w, psum))
             before = tuple(resid[1:-1])
         return before, psum, w
 
-    carry = lax.fori_loop(
-        0, groups - 1, lambda i, c: group_step(i, c, False), carry
-    )
-    _, _, w = group_step(groups - 1, carry, True)
-    for t in range(4):
-        w_ref[count, t] = w[t]
-    share = [w[t] * (1.0 / (count + 1)) for t in (1, 2)]
-
-    def square_step(i, total):
+    opening = residual(fetch_extra(refs, 0), fetch(refs, 0, 0), fetch_extra(refs, 2))
+    carry = tuple(opening[1:-1]), (zero,) * 4, (zero,) * 4
+    carry = lax.fori_loop(0, groups - 1, lambda i, c: first_group(i, c, False), carry)
+    w = first_group(groups - 1, carry, True)[2]
+
+    gy, rank = lax.axis_index("gy"), lax.axis_index("img")
+    final = lax.axis_size("gy") - 1
+    opens = (gy == 0) & (rank == order[0])
+    closes = (gy == final) & (rank == (order[0] if final % 2 else order[-1]))
+    whole = jnp.float32(time_step * time_step)
+    none = jnp.float32(0.0)
+    keep = [jnp.where(opens, none, whole), whole, whole, jnp.where(closes, none, whole)]
+    share = [v * (1.0 / (count + 1)) for v in w]
+
+    def update_group(i, peak):
         for m in range(per):
             k = i * per + m
             at = (k + 1).astype(jnp.float32)
-            for n, t in enumerate((1, 2)):
-                u = time_step * time_step * (w_ref[k, t] - at * share[n])
-                total = total + u * u
-        return total
-
-    total = lax.fori_loop(0, groups, square_step, zero)
-    line = jnp.sum(total, axis=0, keepdims=True)
+            for t in range(4):
+                u = keep[t] * (w_ref[k, t] - at * share[t])
+                w_ref[k, t] = u
+                peak = jnp.maximum(peak, jnp.abs(u))
+                if t in (1, 2):
+                    field_ref[k, t - 1] = u
+        return peak
+
+    peak = lax.fori_loop(0, groups, update_group, zero)
+    for t in range(4):
+        w_ref[count, t] = zero
+    sigma = jnp.maximum(jnp.max(peak), jnp.float32(1e-30))
+    inverse = 1.0 / sigma
+
+    def second_group(i, carry):
+        v, before, psum, w = carry
+        mob = fetch_extra(refs, 2)[1:-1]
+        for m in range(per):
+            k = i * per + m
+            path = fetch(refs, i, 2 * m)[1:-1]
+            ahead = [w_ref[k + 1, t] * inverse for t in range(4)]
+            r1, m1, m2, m3, r2, r3 = [], [], [], [], [], []
+            for t, q in enumerate(lap(pad_zero(v))):
+                a, b, p = v[t], mob[t], path[t]
+                one = b * (stiffness * q + a - 3.0 * p * p * a) - slope * (ahead[t] - a)
+                ba = b * a
+                two = 3.0 * p * a * ba
+                three = -a * a * ba
+                r1.append(one)
+                r2.append(two)
+                r3.append(three)
+                m1.append(b * one)
+                m2.append(b * two)
+                m3.append(b * three)
+            l1, l2, l3 = lap(m1), lap(m2), lap(m3)
+            grads, later = [], []
+            for t in range(2):
+                a, p, m0 = v[t + 1], path[t + 1], mres_ref[k, t]
+                e0, e1, e2 = 1.0 - 3.0 * p * p, 6.0 * p * a, -3.0 * a * a
+                n1, n2, n3 = m1[t + 1], m2[t + 1], m3[t + 1]
+                s1, s2, s3 = r1[t + 1], r2[t + 1], r3[t + 1]
+                b1, b2, b3 = before[t]
+                grads.append((
+                    slope * (b1 - s1) - stiffness * l1[t] - (e0 * n1 + e1 * m0),
+                    slope * (b2 - s2) - stiffness * l2[t] - (e0 * n2 + e1 * n1 + e2 * m0),
+                    slope * (b3 - s3) - stiffness * l3[t] - (e0 * n3 + e1 * n2 + e2 * n1),
+                    -(e1 * n3 + e2 * n2),
+                    -(e2 * n3),
+                ))
+                later.append((s1, s2, s3))
+            for t in range(2):
+                for n in range(DEGREE):
+                    field_ref[k, 2 * n + 2 + t] = w[t][n]
+            psum = tuple(tuple(p + g for p, g in zip(psum[t], grads[t])) for t in range(2))
+            w = tuple(tuple(a - p for a, p in zip(w[t], psum[t])) for t in range(2))
+            before = tuple(later)
+            v = tuple(ahead)
+        return v, before, psum, w
+
+    v = tuple(w_ref[0, t] * inverse for t in range(4))
+    before = tuple((-slope * v[t + 1], zero, zero) for t in range(2))
+    carry = v, before, ((zero,) * DEGREE,) * 2, ((zero,) * DEGREE,) * 2
+    w = lax.fori_loop(0, groups, second_group, carry)[3]
+    share = [[a * (1.0 / (count + 1)) for a in w[t]] for t in range(2)]
+
+    def square_group(i, total):
+        total = list(total)
+        for m in range(per):
+            k = i * per + m
+            at = (k + 1).astype(jnp.float32)
+            for t in range(2):
+                f = [field_ref[k, t]]
+                for n in range(DEGREE):
+                    u = whole * (field_ref[k, 2 * n + 2 + t] - at * share[t][n])
+                    field_ref[k, 2 * n + 2 + t] = u
+                    f.append(u)
+                for n in range(2 * DEGREE + 1):
+                    low = [(a, n - a) for a in range(DEGREE + 1) if a < n - a <= DEGREE]
+                    if low:
+                        cross = functools.reduce(lambda x, y: x + y, [f[a] * f[b] for a, b in low])
+                        cross = cross + cross
+                        if n % 2 == 0:
+                            cross = cross + f[n // 2] * f[n // 2]
+                    else:
+                        cross = f[n // 2] * f[n // 2]
+                    total[n] = total[n] + cross
+        return tuple(total)
+
+    total = lax.fori_loop(0, groups, square_group, (zero,) * (2 * DEGREE + 1))
+    rows = [jnp.sum(v, axis=0, keepdims=True) for v in total]
+    rows += [jnp.zeros_like(rows[0])] * (16 - len(rows))
+    sums = jnp.sum(jnp.concatenate(rows, 0), axis=1, keepdims=True)
+    where_to = lax.broadcasted_iota(jnp.int32, (16, shape[1]), 0)
+    lane = lax.broadcasted_iota(jnp.int32, (16, shape[1]), 1)
+    line = jnp.sum(jnp.where(lane == where_to, sums, 0.0), axis=0, keepdims=True)
+    line = jnp.where(lane[:1] == 2 * DEGREE + 1, sigma, line)
     part_ref[...] = jnp.broadcast_to(line, part_ref.shape)
 
 
-def second_kernel(cells, order, own_ref, prev_ref, next_ref, w_ref, parts_ref, out_ref, part_ref):
-    refs = (prev_ref, own_ref, next_ref)
-    groups, per = own_ref.shape[0], own_ref.shape[1] // 2
-    count = groups * per
-    shape = own_ref.shape[2:]
-    even = row_parity(shape)
-    scale = step_length * lax.rsqrt(jnp.sum(parts_ref[...]) / cells + 1e-06)
-    scale = scale * (time_step * time_step)
-    gy, rank = lax.axis_index("gy"), lax.axis_index("img")
-    flip = lax.rem(gy, 2)
-    opens = (gy == 0) & (rank == order[0])
-    final = lax.axis_size("gy") - 1
-    last_rank = order[0] if final % 2 else order[-1]
-    closes = (gy == final) & (rank == last_rank)
-    none = jnp.float32(0.0)
-    scales = [jnp.where(opens, none, scale), scale, scale, jnp.where(closes, none, scale)]
-    share = [w_ref[count, t] * (1.0 / (count + 1)) for t in range(4)]
-
-    def moved(i, m):
-        k = i * per + m
-        at = jnp.asarray(k + 1, jnp.int32).astype(jnp.float32)
-        tiles = fetch(refs, i, 2 * m)[1:-1]
-        return [v - s * (w_ref[k, t] - at * c) for t, (v, s, c) in enumerate(zip(tiles, scales, share))]
-
-    mob = fetch_extra(refs, 2)[1:-1]
-    start = fetch_extra(refs, 0)[1:-1]
-    now = moved(0, 0)
-    r0 = residual(start, now, mob, even)
-    zero = jnp.zeros(shape, jnp.float32)
-    carry = tuple(now), tuple(r0[1:-1]), (zero,) * 2, (zero,) * 2
-
-    def group_step(i, carry, last_group):
-        now, before, psum, w = carry
-        for m in range(per):
-            if m < per - 1:
-                ahead = moved(i, m + 1)
-            elif last_group:
-                ahead = fetch_extra(refs, 1)[1:-1]
-            else:
-                ahead = moved(i + 1, 0)
-            resid = residual(now, ahead, mob, even)
-            grad = gradient(now, before, resid, mob, even)
-            for t in range(2):
-                out_ref[i, 4 * m + t] = now[t + 1]
-                out_ref[i, 4 * m + 2 + t] = w[t]
-            psum = tuple(p + g for p, g in zip(psum, grad))
-            w = tuple(a - p for a, p in zip(w, psum))
-            before = tuple(resid[1:-1])
-            now = tuple(ahead)
-        return now, before, psum, w
-
-    carry = lax.fori_loop(
-        0, groups - 1, lambda i, c: group_step(i, c, False), carry
-    )
-    w = group_step(groups - 1, carry, True)[3]
-    share = [v * (1.0 / (count + 1)) for v in w]
-
-    def square_step(i, total):
-        for m in range(per):
-            at = (i * per + m + 1).astype(jnp.float32)
-            for t in range(2):
-                u = time_step * time_step * (out_ref[i, 4 * m + 2 + t] - at * share[t])
-                out_ref[i, 4 * m + 2 + t] = u
-                total = total + u * u
-        return total
-
-    total = lax.fori_loop(0, groups, square_step, zero)
-    line = jnp.sum(total, axis=0, keepdims=True)
-    part_ref[...] = jnp.broadcast_to(line, part_ref.shape)
-
-
-def last_kernel(cells, data_ref, parts_ref, out_ref):
+def last_kernel(cells, own_ref, field_ref, part_ref, parts_ref, out_ref):
     groups, per = out_ref.shape[0], out_ref.shape[1] // 2
-    scale = step_length * lax.rsqrt(jnp.sum(parts_ref[...]) / cells + 1e-06)
+    parts = parts_ref[...]
+    lane = lax.broadcasted_iota(jnp.int32, parts.shape, 1)
+    zero = jnp.float32(0.0)
+    at_sigma = 2 * DEGREE + 1
+
+    def scale_of(squares):
+        return step_length * lax.rsqrt(squares / cells + 1e-06)
+
+    first = scale_of(jnp.sum(jnp.where(lane == 0, parts, zero)))
+    sigmas = jnp.sum(jnp.where(lane == at_sigma, parts, zero), axis=1, keepdims=True)
+    power = jnp.broadcast_to(first * sigmas, parts.shape)
+    terms = jnp.where(lane < at_sigma, parts, zero)
+    for bit in range(4):
+        terms = jnp.where((lane >> bit) & 1 == 1, terms * power, terms)
+        power = power * power
+    second = scale_of(jnp.maximum(jnp.sum(terms), zero))
+    mine = part_ref[:1, :]
+    x = first * jnp.sum(jnp.where(lane[:1] == at_sigma, mine, zero))
     for i in range(groups):
         for m in range(per):
+            k = i * per + m
             for t in range(2):
-                out_ref[i, 2 * m + t] = data_ref[i, 4 * m + t] - scale * data_ref[i, 4 * m + 2 + t]
+                u = field_ref[k, t]
+                total = field_ref[k, 2 * DEGREE + t]
+                for n in range(DEGREE - 1, -1, -1):
+                    total = total * x + field_ref[k, 2 * n + t]
+                out_ref[i, 2 * m + t] = own_ref[i, 2 * m + t] - first * u - second * total
 
 
 def unpack_kernel(order, data_ref, out_ref):
@@ -368,7 +411,7 @@
 WHOLE_VMEM = 67043328
 
 
-def call(kernel, outs, count, scalars=0, limit=VMEM_LIMIT):
+def call(kernel, outs, count, scalars=0, scratch=(), limit=VMEM_LIMIT):
     shapes = [jax.ShapeDtypeStruct(s, jnp.float32) for s in outs]
     places = [pl.BlockSpec(memory_space=pltpu.VMEM) for _ in outs]
     single = len(outs) == 1
@@ -378,6 +421,7 @@
         in_specs=[pl.BlockSpec(memory_space=pltpu.VMEM)] * count
         + [pl.BlockSpec(memory_space=pltpu.SMEM)] * scalars,
         out_specs=places[0] if single else places,
+        scratch_shapes=[pltpu.VMEM(shape, jnp.float32) for shape in scratch],
         compiler_params=pltpu.CompilerParams(vmem_limit_bytes=limit),
     )
 
@@ -408,18 +452,15 @@
     own = swap(packed, "img")
     prev = lax.ppermute(own, both, ahead)
     after = lax.ppermute(own, both, back)
-    w, part = call(first_kernel, [(images * groups + 1, 4) + tile, (every, lanes)], 3)(
-        own, prev, after
-    )
+    field, part = call(
+        functools.partial(iterations_kernel, order),
+        [(images * groups, 2 * DEGREE + 2) + tile, (every, lanes)],
+        3,
+        scratch=[(images * groups + 1, 4) + tile, (images * groups, 2) + tile],
+    )(own, prev, after)
     parts = swap(part, both)
-    moved, part = call(
-        functools.partial(second_kernel, cells, order),
-        [(groups, 4 * images) + tile, (every, lanes)],
-        5,
-    )(own, prev, after, w, parts)
-    parts = swap(part, both)
-    done = call(functools.partial(last_kernel, cells), [(groups, 2 * images) + tile], 2)(
-        moved, parts
+    done = call(functools.partial(last_kernel, cells), [(groups, 2 * images) + tile], 4)(
+        own, field, part, parts
     )
     home = swap(done, "img")
     return call(functools.partial(unpack_kernel, order), [path.shape], 1)(home)

time: 65.8 us -> 57.9 us (0.88)
  blocking collectives: 47.9 us -> 39 us
  Pallas kernels: 6.27 us -> 7.2 us
    all_to_all x4 -> x3, blocking collectives: 47.9 us -> 39 us  [swap(): return lax.all_to_all(v, axis, split_axis=0, concat_axis=0, tiled=True)]
    pallas_call x2 -> x1, Pallas kernels: 3.45 us -> 4.12 us  [blocked(): call(functools.partial(iterations_kernel, order), [(images * groups, 2 *...]
where the time goes in v3:
time: 57.9 us; the launch traced here: 57.5 us
  blocking collectives  39 us (67%)
  Pallas kernels  7.2 us (12%)
  starting transfers between devices  5.84 us (10%)
  waiting for transfers between devices  5.44 us (9%)
    all_to_all x3, blocking collectives, swap(): return lax.all_to_all(v, axis, split_axis=0, concat_axis=0, tiled=True)  39 us
    ppermute x1, waiting for transfers between devices, blocked(): after = lax.ppermute(own, both, back)  5.44 us
    ppermute x1, starting transfers between devices, blocked(): prev = lax.ppermute(own, both, ahead)  4.56 us
    pallas_call x1, Pallas kernels, blocked(): call(functools.partial(iterations_kernel, order), [(images * groups, 2 *...  4.12 us
    pallas_call x1, Pallas kernels, blocked(): call(functools.partial(pack_kernel, order), [(groups, 2 * images + 1) + t...  1.85 us
    ppermute x1, starting transfers between devices, blocked(): after = lax.ppermute(own, both, back)  1.28 us
  transfers between devices with their start and end apart: 2, of which 1 were waited for; matrix products, arithmetic and copies ran while one was open for 0% of the time, Pallas kernels for 0%

profile of v3, /device:TPU:0, one launch (start us, length us, event | category | flops | bytes accessed | tf_op | source)
XLA Modules:
  0.0 57.5 jit_solution(14719972309213952793)
XLA Ops:
  0.0 1.8 %shard_map.55 = f32[8,9,8,128]{3,2,1,0:T(8,128)} custom-call(f32[4,4,32,128]{3,2,1,0:T(8,128)} %path_ref.1, f32[4,32,128]{2,1,0:T(8,128)} %start_ref.1, f32[4,32,128]{2,1,0:T(8,128)} %end_ref.1, s32[4,32,128]{2,1,0:T(8,128)} %labels_ref.1, f32[4]{0:T(128)} %table_ref.1), custom_call_target="tpu_custom_call" | custom-call | tf_op jit(solution)/shard_map/pallas_call | solution.py:445
  1.8 17.6 %all_to_all.21.own_ref = f32[8,9,8,128]{3,2,1,0:T(8,128)S(1)} all-to-all(f32[8,9,8,128]{3,2,1,0:T(8,128)} %shard_map.55), channel_id=1, replica_groups=mesh['img'=8,'gy'=4] {'img'}, dimensions={0} | all-to-all | bytes 589824 | tf_op jit(solution)/shard_map/all_to_all | solution.py:443
  19.5 1.3 %collective-permute-start.1 = (f32[8,9,8,128]{3,2,1,0:T(8,128)S(1)}, f32[8,9,8,128]{3,2,1,0:T(8,128)S(1)}, u32[]{:S(2)}, u32[]{:S(2)}) collective-permute-start(f32[8,9,8,128]{3,2,1,0:T(8,128)S(1)} %all_to_all.21.own_ref), channel_id=1, source_target_pairs={{4,0},{12,4},{8,12},{16,8},{20,16},{28,20},{24,28},{25,24},{29,25}... | collective-permute-start | bytes 884744 | tf_op jit(solution)/shard_map/ppermute | solution.py:454
  20.8 4.6 %collective-permute-start = (f32[8,9,8,128]{3,2,1,0:T(8,128)S(1)}, f32[8,9,8,128]{3,2,1,0:T(8,128)S(1)}, u32[]{:S(2)}, u32[]{:S(2)}) collective-permute-start(f32[8,9,8,128]{3,2,1,0:T(8,128)S(1)} %all_to_all.21.own_ref), channel_id=1, source_target_pairs={{0,4},{4,12},{12,8},{8,16},{16,20},{20,28},{28,24},{24,25},{25,29}... | collective-permute-start | bytes 884744 | tf_op jit(solution)/shard_map/ppermute | solution.py:453
  25.4 5.4 %collective-permute-done.1.next_ref = f32[8,9,8,128]{3,2,1,0:T(8,128)S(1)} collective-permute-done((f32[8,9,8,128]{3,2,1,0:T(8,128)S(1)}, f32[8,9,8,128]{3,2,1,0:T(8,128)S(1)}, u32[]{:S(2)}, u32[]{:S(2)}) %collective-permute-start.1) | collective-permute-done | bytes 294944 | tf_op jit(solution)/shard_map/ppermute | solution.py:454
  30.8 0.0 collective-permute-done.prev_ref
  30.8 4.1 %shard_map.56 = (f32[32,12,8,128]{3,2,1,0:T(8,128)S(1)}, f32[32,128]{1,0:T(8,128)S(1)}) custom-call(f32[8,9,8,128]{3,2,1,0:T(8,128)S(1)} %all_to_all.21.own_ref, f32[8,9,8,128]{3,2,1,0:T(8,128)S(1)} %collective-permute-done.prev_ref, f32[8,9,8,128]{3,2,1,0:T(8,128)S(1)} %collective-permute-done.1.next_ref), custom_call_target="tpu_custom_call" | custom-call | tf_op jit(solution)/shard_map/pallas_call | solution.py:455
  34.9 9.7 %all_to_all.22 = f32[32,1,128]{2,1,0:T(1,128)S(1)} all-to-all(f32[32,1,128]{2,1,0:T(1,128)S(1)} %bitcast.4), channel_id=1, replica_groups=mesh['img'=8,'gy'=4] {'img','gy'}, dimensions={0} | all-to-all | bytes 32768 | tf_op jit(solution)/shard_map/all_to_all | solution.py:443
  44.7 0.4 shard_map.57
  45.1 11.6 %all_to_all.23.data_ref = f32[8,8,8,128]{3,2,1,0:T(8,128)S(1)} all-to-all(f32[8,8,8,128]{3,2,1,0:T(8,128)S(1)} %shard_map.57), channel_id=1, replica_groups=mesh['img'=8,'gy'=4] {'img'}, dimensions={0} | all-to-all | bytes 524288 | tf_op jit(solution)/shard_map/all_to_all | solution.py:443
  56.8 0.8 %shard_map.58 = f32[4,4,32,128]{3,2,1,0:T(8,128)} custom-call(f32[8,8,8,128]{3,2,1,0:T(8,128)S(1)} %all_to_all.23.data_ref), custom_call_target="tpu_custom_call" | custom-call | tf_op jit(solution)/shard_map/pallas_call | solution.py:466
Async XLA Ops:
  19.5 11.3 %collective-permute-start.1 = (f32[8,9,8,128]{3,2,1,0:T(8,128)S(1)}, f32[8,9,8,128]{3,2,1,0:T(8,128)S(1)}, u32[]{:S(2)}, u32[]{:S(2)}) collective-permute-start(f32[8,9,8,128]{3,2,1,0:T(8,128)S(1)} %all_to_all.21.own_ref), channel_id=1, source_target_pairs={{4,0},{12,4},{8,12},{16,8},{20,16},{28,20},{24,28},{25,24},{29,25}... | collective-permute-start | bytes 884744 | tf_op jit(solution)/shard_map/ppermute | solution.py:454
  20.8 10.0 %collective-permute-start = (f32[8,9,8,128]{3,2,1,0:T(8,128)S(1)}, f32[8,9,8,128]{3,2,1,0:T(8,128)S(1)}, u32[]{:S(2)}, u32[]{:S(2)}) collective-permute-start(f32[8,9,8,128]{3,2,1,0:T(8,128)S(1)} %all_to_all.21.own_ref), channel_id=1, source_target_pairs={{0,4},{4,12},{12,8},{8,16},{16,20},{20,28},{28,24},{24,25},{25,29}... | collective-permute-start | bytes 884744 | tf_op jit(solution)/shard_map/ppermute | solution.py:453

commit v4 on v3

--- a/solution.py
+++ b/solution.py
@@ -99,44 +99,74 @@
     return path
 
 
-def walk(mesh):
-    count = mesh.shape["img"]
+def walks(mesh):
+    count, slabs = mesh.shape["img"], mesh.shape["gy"]
     plain = list(range(count))
+    plan = [plain if g % 2 == 0 else plain[::-1] for g in range(slabs)]
     try:
         line = mesh.devices.reshape(count, -1)[:, 0]
         place = [tuple(d.coords) for d in line]
     except Exception:
-        return plain
-
-    def near(a, b):
-        return sum(abs(p - q) for p, q in zip(place[a], place[b])) <= 1
-
-    def grow(order):
+        return plan
+
+    def step(a, b):
+        moved = [n for n, (p, q) in enumerate(zip(place[a], place[b])) if p != q]
+        near = sum(abs(p - q) for p, q in zip(place[a], place[b])) <= 1
+        return (moved[0] if moved else -1) if near else None
+
+    def grow(order, sign):
         if len(order) == count:
             return order
-        for nxt in plain:
-            if nxt not in order and near(order[-1], nxt):
-                found = grow(order + [nxt])
-                if found:
-                    return found
+        options = [n for n in plain if n not in order and step(order[-1], n) is not None]
+        for nxt in sorted(options, key=lambda n: sign * step(order[-1], n)):
+            found = grow(order + [nxt], sign)
+            if found:
+                return found
         return None
 
-    return grow([0]) or plain
-
-
-def spread(order, position, flip):
-    return jnp.where(flip == 1, order[len(order) - 1 - position], order[position])
-
-
-def pack_kernel(order, path_ref, start_ref, end_ref, labels_ref, table_ref, out_ref):
+    found, start = [], 0
+    for g in range(slabs):
+        order = grow([start], 1 if g % 2 == 0 else -1)
+        if not order:
+            return plan
+        found.append(order)
+        start = order[-1]
+    return found
+
+
+def picked(options, index):
+    out = jnp.asarray(options[0], jnp.int32)
+    for n, v in enumerate(options[1:], 1):
+        out = jnp.where(index == n, jnp.asarray(v, jnp.int32), out)
+    return out
+
+
+def holder(orders, position):
+    return picked([order[position] for order in orders], lax.axis_index("gy"))
+
+
+def block_here(orders):
+    rank, gy = lax.axis_index("img"), lax.axis_index("gy")
+    inverse = [[order.index(n) for n in range(len(order))] for order in orders]
+    return picked([picked(places, rank) for places in inverse], gy)
+
+
+def pack_kernel(orders, path_ref, start_ref, end_ref, labels_ref, table_ref, out_ref):
     images, planes, rows, lanes = path_ref.shape
-    groups = len(order)
-    flip = lax.rem(lax.axis_index("gy"), 2)
+    groups = len(orders[0])
     rank = lax.axis_index("img")
     slab = rank // 2
     odd = lax.rem(rank, 2) == 1
+    slabs = []
+    for x in range(planes):
+        label = labels_ref[x]
+        mob = jnp.zeros(label.shape, jnp.float32)
+        for level in range(table_ref.shape[0]):
+            mob = mob + jnp.where(label == level, table_ref[level], jnp.float32(0.0))
+        ends = jnp.where(slab == 0, start_ref[x], end_ref[x])
+        slabs.append(jnp.where(slab >= 2, mob, ends))
     for c in range(groups):
-        dest = spread(order, c, flip)
+        dest = holder(orders, c)
         for m in range(images):
             for h in range(2):
                 row = 4 * c + 2 * h
@@ -145,21 +175,11 @@
         extra = []
         for h in range(2):
             row = 4 * c + 2 * h
-
-            def tile(ref):
-                parts = [ref[x, row : row + 2, :] for x in range(planes)]
-                return jnp.concatenate(parts, 0)
-
-            label = tile(labels_ref)
-            mob = jnp.zeros(label.shape, jnp.float32)
-            for level in range(table_ref.shape[0]):
-                mob = mob + jnp.where(label == level, table_ref[level], jnp.float32(0.0))
-            ends = jnp.where(slab == 0, tile(start_ref), tile(end_ref))
-            extra.append(jnp.where(slab >= 2, mob, ends))
+            extra.append(jnp.concatenate([v[row : row + 2, :] for v in slabs], 0))
         out_ref[dest, 2 * images] = jnp.where(odd, extra[1], extra[0])
 
 
-def lap(tiles):
+def around(tiles):
     sublanes, lanes = tiles[0].shape
     r_is_0 = lax.rem(lax.broadcasted_iota(jnp.int32, tiles[0].shape, 0), 2) == 0
     out = []
@@ -167,9 +187,9 @@
     for h in range(1, len(tiles) - 1):
         v = tiles[h]
         total = pltpu.roll(v, 2, 0) + pltpu.roll(v, sublanes - 2, 0)
-        total = total + pltpu.roll(v, 1, 1) + pltpu.roll(v, lanes - 1, 1)
+        total = total + (pltpu.roll(v, 1, 1) + pltpu.roll(v, lanes - 1, 1))
         lower, upper = pltpu.roll(pair[h - 1], sublanes - 1, 0), pltpu.roll(pair[h], 1, 0)
-        out.append(total + jnp.where(r_is_0, lower, upper) - 6.0 * v)
+        out.append(total + jnp.where(r_is_0, lower, upper))
     return out
 
 
@@ -178,20 +198,23 @@
     return [zero] + list(tiles) + [zero]
 
 
-def residual(now, ahead, mob):
+FLAT = 6.0 - 1.0 / stiffness
+BENT = 1.0 / stiffness
+
+
+def residual(now, ahead, scaled):
     out = []
-    for v, w, q, m in zip(now, ahead, lap(pad_zero(now)), mob):
-        force = m * (stiffness * q + v - v * v * v)
-        out.append((w - v) * (1.0 / time_step) - force)
+    for v, w, q, c in zip(now, ahead, around(pad_zero(now)), scaled):
+        out.append((w - v) - c * (q - v * (FLAT + BENT * (v * v))))
     return out
 
 
 def gradient(now, before, resid, mres):
     out = []
-    for n, q in enumerate(lap(mres)):
+    for n, q in enumerate(around(mres)):
         v = now[n + 1]
-        adjoint = stiffness * q + (1.0 - 3.0 * v * v) * mres[n + 1]
-        out.append((before[n] - resid[n + 1]) * (1.0 / time_step) - adjoint)
+        own = mres[n + 1] * (FLAT + 3.0 * BENT * (v * v))
+        out.append((before[n] - resid[n + 1]) - (q - own))
     return out
 
 
@@ -213,28 +236,43 @@
 DEGREE = 5
 
 
-def iterations_kernel(order, own_ref, prev_ref, next_ref, field_ref, part_ref, w_ref, mres_ref):
+def iterations_kernel(
+    orders, own_ref, prev_ref, next_ref, field_ref, part_ref, w_ref, mres_ref, scaled_ref
+):
     refs = (prev_ref, own_ref, next_ref)
     groups, per = own_ref.shape[0], own_ref.shape[1] // 2
     count = groups * per
     shape = own_ref.shape[2:]
     zero = jnp.zeros(shape, jnp.float32)
-    slope = 1.0 / time_step
+    gy, block = lax.axis_index("gy"), block_here(orders)
+    none, whole = jnp.float32(0.0), jnp.float32(1.0)
+    lower = jnp.where((gy == 0) & (block == 0), none, whole)
+    upper = jnp.where((gy == lax.axis_size("gy") - 1) & (block == groups - 1), none, whole)
+    inside = [lower, lower, None, None, upper, upper]
+
+    def masked(value, mask):
+        return value if mask is None else mask * value
+
+    for t, v in enumerate(fetch_extra(refs, 2)):
+        scaled_ref[t] = masked((time_step * stiffness) * v, inside[t])
+
+    def known(tiles):
+        return [masked(v, inside[t]) if t in (1, 4) else v for t, v in enumerate(tiles)]
 
     def first_group(i, carry, last_group):
         before, psum, w = carry
-        mob = fetch_extra(refs, 2)
+        scaled = [scaled_ref[t] for t in range(6)]
         for m in range(per):
             k = i * per + m
-            now = fetch(refs, i, 2 * m)
+            now = known(fetch(refs, i, 2 * m))
             if m < per - 1:
                 ahead = fetch(refs, i, 2 * m + 2)
             elif last_group:
                 ahead = fetch_extra(refs, 1)
             else:
                 ahead = fetch(refs, i + 1, 0)
-            resid = residual(now, ahead, mob)
-            mres = [a * b for a, b in zip(mob, resid)]
+            resid = residual(now, ahead, scaled)
+            mres = [a * b for a, b in zip(scaled, resid)]
             grad = gradient(now, before, resid, mres)
             for t in range(4):
                 w_ref[k, t] = w[t]
@@ -245,18 +283,12 @@
             before = tuple(resid[1:-1])
         return before, psum, w
 
-    opening = residual(fetch_extra(refs, 0), fetch(refs, 0, 0), fetch_extra(refs, 2))
+    scaled = [scaled_ref[t] for t in range(6)]
+    opening = residual(known(fetch_extra(refs, 0)), fetch(refs, 0, 0), scaled)
     carry = tuple(opening[1:-1]), (zero,) * 4, (zero,) * 4
     carry = lax.fori_loop(0, groups - 1, lambda i, c: first_group(i, c, False), carry)
     w = first_group(groups - 1, carry, True)[2]
 
-    gy, rank = lax.axis_index("gy"), lax.axis_index("img")
-    final = lax.axis_size("gy") - 1
-    opens = (gy == 0) & (rank == order[0])
-    closes = (gy == final) & (rank == (order[0] if final % 2 else order[-1]))
-    whole = jnp.float32(time_step * time_step)
-    none = jnp.float32(0.0)
-    keep = [jnp.where(opens, none, whole), whole, whole, jnp.where(closes, none, whole)]
     share = [v * (1.0 / (count + 1)) for v in w]
 
     def update_group(i, peak):
@@ -264,7 +296,7 @@
             k = i * per + m
             at = (k + 1).astype(jnp.float32)
             for t in range(4):
-                u = keep[t] * (w_ref[k, t] - at * share[t])
+                u = masked(w_ref[k, t] - at * share[t], inside[t + 1])
                 w_ref[k, t] = u
                 peak = jnp.maximum(peak, jnp.abs(u))
                 if t in (1, 2):
@@ -279,38 +311,43 @@
 
     def second_group(i, carry):
         v, before, psum, w = carry
-        mob = fetch_extra(refs, 2)[1:-1]
+        scaled = [scaled_ref[t + 1] for t in range(4)]
         for m in range(per):
             k = i * per + m
             path = fetch(refs, i, 2 * m)[1:-1]
             ahead = [w_ref[k + 1, t] * inverse for t in range(4)]
-            r1, m1, m2, m3, r2, r3 = [], [], [], [], [], []
-            for t, q in enumerate(lap(pad_zero(v))):
-                a, b, p = v[t], mob[t], path[t]
-                one = b * (stiffness * q + a - 3.0 * p * p * a) - slope * (ahead[t] - a)
-                ba = b * a
-                two = 3.0 * p * a * ba
-                three = -a * a * ba
+            r1, r2, r3, m1, m2, m3 = [], [], [], [], [], []
+            squares = []
+            for t, q in enumerate(around(pad_zero(v))):
+                a, c, p = v[t], scaled[t], path[t]
+                pull = FLAT + 3.0 * BENT * (p * p)
+                ca = c * a
+                cross = (3.0 * BENT) * (p * a)
+                bend = BENT * (a * a)
+                one = c * (q - a * pull) - (ahead[t] - a)
+                two = cross * ca
+                three = bend * ca
                 r1.append(one)
                 r2.append(two)
                 r3.append(three)
-                m1.append(b * one)
-                m2.append(b * two)
-                m3.append(b * three)
-            l1, l2, l3 = lap(m1), lap(m2), lap(m3)
+                m1.append(c * one)
+                m2.append(c * two)
+                m3.append(c * three)
+                squares.append((pull, cross + cross, 3.0 * bend))
+            q1, q2, q3 = around(m1), around(m2), around(m3)
             grads, later = [], []
             for t in range(2):
-                a, p, m0 = v[t + 1], path[t + 1], mres_ref[k, t]
-                e0, e1, e2 = 1.0 - 3.0 * p * p, 6.0 * p * a, -3.0 * a * a
+                pull, cross, bend = squares[t + 1]
+                m0 = mres_ref[k, t]
                 n1, n2, n3 = m1[t + 1], m2[t + 1], m3[t + 1]
                 s1, s2, s3 = r1[t + 1], r2[t + 1], r3[t + 1]
                 b1, b2, b3 = before[t]
                 grads.append((
-                    slope * (b1 - s1) - stiffness * l1[t] - (e0 * n1 + e1 * m0),
-                    slope * (b2 - s2) - stiffness * l2[t] - (e0 * n2 + e1 * n1 + e2 * m0),
-                    slope * (b3 - s3) - stiffness * l3[t] - (e0 * n3 + e1 * n2 + e2 * n1),
-                    -(e1 * n3 + e2 * n2),
-                    -(e2 * n3),
+                    (b1 - s1) - (q1[t] - pull * n1) - cross * m0,
+                    (b2 - s2) - (q2[t] - pull * n2) - (cross * n1 - bend * m0),
+                    (s3 - b3) + (q3[t] - pull * n3) - (cross * n2 - bend * n1),
+                    cross * n3 + bend * n2,
+                    -(bend * n3),
                 ))
                 later.append((s1, s2, s3))
             for t in range(2):
@@ -323,7 +360,7 @@
         return v, before, psum, w
 
     v = tuple(w_ref[0, t] * inverse for t in range(4))
-    before = tuple((-slope * v[t + 1], zero, zero) for t in range(2))
+    before = tuple((-v[t + 1], zero, zero) for t in range(2))
     carry = v, before, ((zero,) * DEGREE,) * 2, ((zero,) * DEGREE,) * 2
     w = lax.fori_loop(0, groups, second_group, carry)[3]
     share = [[a * (1.0 / (count + 1)) for a in w[t]] for t in range(2)]
@@ -336,7 +373,7 @@
             for t in range(2):
                 f = [field_ref[k, t]]
                 for n in range(DEGREE):
-                    u = whole * (field_ref[k, 2 * n + 2 + t] - at * share[t][n])
+                    u = field_ref[k, 2 * n + 2 + t] - at * share[t][n]
                     field_ref[k, 2 * n + 2 + t] = u
                     f.append(u)
                 for n in range(2 * DEGREE + 1):
@@ -393,12 +430,11 @@
                 out_ref[i, 2 * m + t] = own_ref[i, 2 * m + t] - first * u - second * total
 
 
-def unpack_kernel(order, data_ref, out_ref):
+def unpack_kernel(orders, data_ref, out_ref):
     images, planes, rows, lanes = out_ref.shape
-    groups = len(order)
-    flip = lax.rem(lax.axis_index("gy"), 2)
+    groups = len(orders[0])
     for c in range(groups):
-        src = spread(order, c, flip)
+        src = holder(orders, c)
         for m in range(images):
             for h in range(2):
                 row = 4 * c + 2 * h
@@ -426,24 +462,22 @@
     )
 
 
-def blocked(order, path, start_image, end_image, labels, mob_table):
+def blocked(orders, path, start_image, end_image, labels, mob_table):
     images, planes, rows, lanes = path.shape
     groups, slabs = lax.axis_size("img"), lax.axis_size("gy")
     both = ("img", "gy")
     every = groups * slabs
     tile = (2 * planes, lanes)
     cells = images * groups * planes * rows * slabs * lanes
-    line = []
-    for g in range(slabs):
-        line += [i * slabs + g for i in (order[::-1] if g % 2 else order)]
-    ahead = [(line[n], line[n + 1]) for n in range(every - 1)]
+    line = [i * slabs + g for g in range(slabs) for i in orders[g]]
+    ahead = [(line[n - 1], line[n]) for n in range(every)]
     back = [(b, a) for a, b in ahead]
 
     def swap(v, axis):
         return lax.all_to_all(v, axis, split_axis=0, concat_axis=0, tiled=True)
 
     packed = call(
-        functools.partial(pack_kernel, order),
+        functools.partial(pack_kernel, orders),
         [(groups, 2 * images + 1) + tile],
         4,
         scalars=1,
@@ -453,28 +487,32 @@
     prev = lax.ppermute(own, both, ahead)
     after = lax.ppermute(own, both, back)
     field, part = call(
-        functools.partial(iterations_kernel, order),
+        functools.partial(iterations_kernel, orders),
         [(images * groups, 2 * DEGREE + 2) + tile, (every, lanes)],
         3,
-        scratch=[(images * groups + 1, 4) + tile, (images * groups, 2) + tile],
+        scratch=[
+            (images * groups + 1, 4) + tile,
+            (images * groups, 2) + tile,
+            (6,) + tile,
+        ],
     )(own, prev, after)
     parts = swap(part, both)
     done = call(functools.partial(last_kernel, cells), [(groups, 2 * images) + tile], 4)(
         own, field, part, parts
     )
     home = swap(done, "img")
-    return call(functools.partial(unpack_kernel, order), [path.shape], 1)(home)
+    return call(functools.partial(unpack_kernel, orders), [path.shape], 1)(home)
 
 
 def solution(mesh):
-    order = walk(mesh)
+    orders = walks(mesh)
 
     def per_device(path, start_image, end_image, labels, mob_table):
         images, planes, rows, lanes = path.shape
         groups = lax.axis_size("img")
         fits = rows == 4 * groups and planes == 4 and lanes == 128 and groups >= 6
         if fits and ITERS == 2:
-            return blocked(order, path, start_image, end_image, labels, mob_table)
+            return blocked(orders, path, start_image, end_image, labels, mob_table)
         return general(path, start_image, end_image, labels, mob_table)
 
     in_specs = (

time: 57.9 us -> 55.5 us (0.959)
  starting transfers between devices: 5.84 us -> 2.03 us
  blocking collectives: 39 us -> 41.3 us
  waiting for transfers between devices: 5.44 us -> 4.7 us
    ppermute x1, starting transfers between devices: 4.56 us -> 2.02 us  [blocked(): prev = lax.ppermute(own, both, ahead)]
    all_to_all x3, blocking collectives: 39 us -> 41.3 us  [swap(): return lax.all_to_all(v, axis, split_axis=0, concat_axis=0, tiled=True)]
    ppermute x1, starting transfers between devices: 1.28 us -> 0.01 us  [blocked(): after = lax.ppermute(own, both, back)]
    ppermute x1, waiting for transfers between devices: 5.44 us -> 4.7 us  [blocked(): after = lax.ppermute(own, both, back)]
where the time goes in v4:
time: 55.5 us; the launch traced here: 55.2 us
  blocking collectives  41.3 us (74%)
  Pallas kernels  7.15 us (13%)
  waiting for transfers between devices  4.7 us (8%)
  starting transfers between devices  2.03 us (4%)
    all_to_all x3, blocking collectives, swap(): return lax.all_to_all(v, axis, split_axis=0, concat_axis=0, tiled=True)  41.3 us
    ppermute x1, waiting for transfers between devices, blocked(): after = lax.ppermute(own, both, back)  4.7 us
    pallas_call x1, Pallas kernels, blocked(): call(functools.partial(iterations_kernel, orders), [(images * groups, 2 *...  4.11 us
    ppermute x1, starting transfers between devices, blocked(): prev = lax.ppermute(own, both, ahead)  2.02 us
    pallas_call x1, Pallas kernels, blocked(): call(functools.partial(pack_kernel, orders), [(groups, 2 * images + 1) +...  1.81 us
  transfers between devices with their start and end apart: 2, of which 1 were waited for; matrix products, arithmetic and copies ran while one was open for 0% of the time, Pallas kernels for 0%

profile of v4, /device:TPU:0, one launch (start us, length us, event | category | flops | bytes accessed | tf_op | source)
XLA Modules:
  0.0 55.2 jit_solution(11157269342681717501)
XLA Ops:
  0.0 1.8 %shard_map.55 = f32[8,9,8,128]{3,2,1,0:T(8,128)} custom-call(f32[4,4,32,128]{3,2,1,0:T(8,128)} %path_ref.1, f32[4,32,128]{2,1,0:T(8,128)} %start_ref.1, f32[4,32,128]{2,1,0:T(8,128)} %end_ref.1, s32[4,32,128]{2,1,0:T(8,128)} %labels_ref.1, f32[4]{0:T(128)} %table_ref.1), custom_call_target="tpu_custom_call" | custom-call | tf_op jit(solution)/shard_map/pallas_call | solution.py:479
  1.8 17.6 %all_to_all.21.own_ref = f32[8,9,8,128]{3,2,1,0:T(8,128)S(1)} all-to-all(f32[8,9,8,128]{3,2,1,0:T(8,128)} %shard_map.55), channel_id=1, replica_groups=mesh['img'=8,'gy'=4] {'img'}, dimensions={0} | all-to-all | bytes 589824 | tf_op jit(solution)/shard_map/all_to_all | solution.py:477
  19.5 0.0 collective-permute-start.1
  19.5 2.0 %collective-permute-start = (f32[8,9,8,128]{3,2,1,0:T(8,128)S(1)}, f32[8,9,8,128]{3,2,1,0:T(8,128)S(1)}, u32[]{:S(2)}, u32[]{:S(2)}) collective-permute-start(f32[8,9,8,128]{3,2,1,0:T(8,128)S(1)} %all_to_all.21.own_ref), channel_id=1, source_target_pairs={{3,0},{0,4},{4,12},{12,8},{8,16},{16,20},{20,28},{28,24},{24,25},{... | collective-permute-start | bytes 884744 | tf_op jit(solution)/shard_map/ppermute | solution.py:487
  21.5 4.7 %collective-permute-done.1.next_ref = f32[8,9,8,128]{3,2,1,0:T(8,128)S(1)} collective-permute-done((f32[8,9,8,128]{3,2,1,0:T(8,128)S(1)}, f32[8,9,8,128]{3,2,1,0:T(8,128)S(1)}, u32[]{:S(2)}, u32[]{:S(2)}) %collective-permute-start.1) | collective-permute-done | bytes 294944 | tf_op jit(solution)/shard_map/ppermute | solution.py:488
  26.2 0.0 collective-permute-done.prev_ref
  26.2 4.1 %shard_map.56 = (f32[32,12,8,128]{3,2,1,0:T(8,128)S(1)}, f32[32,128]{1,0:T(8,128)S(1)}) custom-call(f32[8,9,8,128]{3,2,1,0:T(8,128)S(1)} %all_to_all.21.own_ref, f32[8,9,8,128]{3,2,1,0:T(8,128)S(1)} %collective-permute-done.prev_ref, f32[8,9,8,128]{3,2,1,0:T(8,128)S(1)} %collective-permute-done.1.next_ref), custom_call_target="tpu_custom_call" | custom-call | tf_op jit(solution)/shard_map/pallas_call | solution.py:489
  30.3 12.0 %all_to_all.22 = f32[32,1,128]{2,1,0:T(1,128)S(1)} all-to-all(f32[32,1,128]{2,1,0:T(1,128)S(1)} %bitcast.4), channel_id=1, replica_groups=mesh['img'=8,'gy'=4] {'img','gy'}, dimensions={0} | all-to-all | bytes 32768 | tf_op jit(solution)/shard_map/all_to_all | solution.py:477
  42.3 0.4 shard_map.57
  42.8 11.6 %all_to_all.23.data_ref = f32[8,8,8,128]{3,2,1,0:T(8,128)S(1)} all-to-all(f32[8,8,8,128]{3,2,1,0:T(8,128)S(1)} %shard_map.57), channel_id=1, replica_groups=mesh['img'=8,'gy'=4] {'img'}, dimensions={0} | all-to-all | bytes 524288 | tf_op jit(solution)/shard_map/all_to_all | solution.py:477
  54.4 0.8 %shard_map.58 = f32[4,4,32,128]{3,2,1,0:T(8,128)} custom-call(f32[8,8,8,128]{3,2,1,0:T(8,128)S(1)} %all_to_all.23.data_ref), custom_call_target="tpu_custom_call" | custom-call | tf_op jit(solution)/shard_map/pallas_call | solution.py:504
Async XLA Ops:
  19.5 6.7 %collective-permute-start.1 = (f32[8,9,8,128]{3,2,1,0:T(8,128)S(1)}, f32[8,9,8,128]{3,2,1,0:T(8,128)S(1)}, u32[]{:S(2)}, u32[]{:S(2)}) collective-permute-start(f32[8,9,8,128]{3,2,1,0:T(8,128)S(1)} %all_to_all.21.own_ref), channel_id=1, source_target_pairs={{0,3},{4,0},{12,4},{8,12},{16,8},{20,16},{28,20},{24,28},{25,24},{... | collective-permute-start | bytes 884744 | tf_op jit(solution)/shard_map/ppermute | solution.py:488
  19.5 6.7 %collective-permute-start = (f32[8,9,8,128]{3,2,1,0:T(8,128)S(1)}, f32[8,9,8,128]{3,2,1,0:T(8,128)S(1)}, u32[]{:S(2)}, u32[]{:S(2)}) collective-permute-start(f32[8,9,8,128]{3,2,1,0:T(8,128)S(1)} %all_to_all.21.own_ref), channel_id=1, source_target_pairs={{3,0},{0,4},{4,12},{12,8},{8,16},{16,20},{20,28},{28,24},{24,25},{... | collective-permute-start | bytes 884744 | tf_op jit(solution)/shard_map/ppermute | solution.py:487

commit v5 on v4

--- a/solution.py
+++ b/solution.py
@@ -151,32 +151,30 @@
     return picked([picked(places, rank) for places in inverse], gy)
 
 
-def pack_kernel(orders, path_ref, start_ref, end_ref, labels_ref, table_ref, out_ref):
+def pack_kernel(orders, path_ref, start_ref, end_ref, labels_ref, table_ref, out_ref, fixed_ref):
     images, planes, rows, lanes = path_ref.shape
-    groups = len(orders[0])
-    rank = lax.axis_index("img")
-    slab = rank // 2
-    odd = lax.rem(rank, 2) == 1
-    slabs = []
-    for x in range(planes):
-        label = labels_ref[x]
-        mob = jnp.zeros(label.shape, jnp.float32)
-        for level in range(table_ref.shape[0]):
-            mob = mob + jnp.where(label == level, table_ref[level], jnp.float32(0.0))
-        ends = jnp.where(slab == 0, start_ref[x], end_ref[x])
-        slabs.append(jnp.where(slab >= 2, mob, ends))
-    for c in range(groups):
+    block = block_here(orders)
+    for c in range(len(orders[0])):
         dest = holder(orders, c)
+
+        def tile(ref, h, *at):
+            row = 4 * c + 2 * h
+            parts = [ref[at + (x, slice(row, row + 2))] for x in range(planes)]
+            return jnp.concatenate(parts, 0)
+
         for m in range(images):
             for h in range(2):
-                row = 4 * c + 2 * h
-                parts = [path_ref[m, x, row : row + 2, :] for x in range(planes)]
-                out_ref[dest, 2 * m + h] = jnp.concatenate(parts, 0)
-        extra = []
-        for h in range(2):
-            row = 4 * c + 2 * h
-            extra.append(jnp.concatenate([v[row : row + 2, :] for v in slabs], 0))
-        out_ref[dest, 2 * images] = jnp.where(odd, extra[1], extra[0])
+                out_ref[dest, 2 * m + h] = tile(path_ref, h, m)
+
+        @pl.when(block == c)
+        def _():
+            for h in range(2):
+                label = tile(labels_ref, h)
+                mob = jnp.zeros(label.shape, jnp.float32)
+                for level in range(table_ref.shape[0]):
+                    mob = mob + jnp.where(label == level, table_ref[level], jnp.float32(0.0))
+                for slab, value in enumerate((tile(start_ref, h), tile(end_ref, h), mob)):
+                    fixed_ref[2 * slab + h] = value
 
 
 def around(tiles):
@@ -225,21 +223,22 @@
     return out
 
 
-def fetch_extra(refs, slab):
-    last = refs[0].shape[1] - 1
-    out = []
-    for ref in refs:
-        out += [ref[2 * slab, last], ref[2 * slab + 1, last]]
-    return out
+def fetch_fixed(refs, slab):
+    before, own, after = refs
+    last = own.shape[0] - 1
+    out = [before[2 * slab], before[2 * slab + 1]]
+    out += [own[last - 2 * slab], own[last - 2 * slab - 1]]
+    return out + [after[2 * slab], after[2 * slab + 1]]
 
 
 DEGREE = 5
 
 
 def iterations_kernel(
-    orders, own_ref, prev_ref, next_ref, field_ref, part_ref, w_ref, mres_ref, scaled_ref
+    orders, own_ref, prev_ref, next_ref, fixed_ref, fixed_prev_ref, fixed_next_ref, field_ref, part_ref, w_ref, mres_ref, scaled_ref
 ):
     refs = (prev_ref, own_ref, next_ref)
+    fixed = (fixed_prev_ref, fixed_ref, fixed_next_ref)
     groups, per = own_ref.shape[0], own_ref.shape[1] // 2
     count = groups * per
     shape = own_ref.shape[2:]
@@ -253,7 +252,7 @@
     def masked(value, mask):
         return value if mask is None else mask * value
 
-    for t, v in enumerate(fetch_extra(refs, 2)):
+    for t, v in enumerate(fetch_fixed(fixed, 2)):
         scaled_ref[t] = masked((time_step * stiffness) * v, inside[t])
 
     def known(tiles):
@@ -268,7 +267,7 @@
             if m < per - 1:
                 ahead = fetch(refs, i, 2 * m + 2)
             elif last_group:
-                ahead = fetch_extra(refs, 1)
+                ahead = fetch_fixed(fixed, 1)
             else:
                 ahead = fetch(refs, i + 1, 0)
             resid = residual(now, ahead, scaled)
@@ -284,7 +283,7 @@
         return before, psum, w
 
     scaled = [scaled_ref[t] for t in range(6)]
-    opening = residual(known(fetch_extra(refs, 0)), fetch(refs, 0, 0), scaled)
+    opening = residual(known(fetch_fixed(fixed, 0)), fetch(refs, 0, 0), scaled)
     carry = tuple(opening[1:-1]), (zero,) * 4, (zero,) * 4
     carry = lax.fori_loop(0, groups - 1, lambda i, c: first_group(i, c, False), carry)
     w = first_group(groups - 1, carry, True)[2]
@@ -476,26 +475,26 @@
     def swap(v, axis):
         return lax.all_to_all(v, axis, split_axis=0, concat_axis=0, tiled=True)
 
-    packed = call(
+    packed, fixed = call(
         functools.partial(pack_kernel, orders),
-        [(groups, 2 * images + 1) + tile],
+        [(groups, 2 * images) + tile, (6,) + tile],
         4,
         scalars=1,
         limit=WHOLE_VMEM,
     )(path, start_image, end_image, labels, mob_table)
     own = swap(packed, "img")
-    prev = lax.ppermute(own, both, ahead)
-    after = lax.ppermute(own, both, back)
+    blocks = [own] + [lax.ppermute(own, both, way) for way in (ahead, back)]
+    blocks += [fixed[::-1]] + [lax.ppermute(fixed, both, way) for way in (ahead, back)]
     field, part = call(
         functools.partial(iterations_kernel, orders),
         [(images * groups, 2 * DEGREE + 2) + tile, (every, lanes)],
-        3,
+        6,
         scratch=[
             (images * groups + 1, 4) + tile,
             (images * groups, 2) + tile,
             (6,) + tile,
         ],
-    )(own, prev, after)
+    )(*blocks)
     parts = swap(part, both)
     done = call(functools.partial(last_kernel, cells), [(groups, 2 * images) + tile], 4)(
         own, field, part, parts

time: 55.5 us -> 54.5 us (0.982)
  waiting for transfers between devices: 4.7 us -> 1.97 us
  starting transfers between devices: 2.03 us -> 4.05 us
  blocking collectives: 41.3 us -> 40.2 us
  local copies, waits for them, and re-layouts: 0 us -> 0.77 us
    ppermute x2 -> x4, waiting for transfers between devices: 4.7 us -> 1.97 us  [the longest x2 1.97 us: blocked(): lax.ppermute(fixed, both, way)]
    ppermute x2 -> x4, starting transfers between devices: 2.03 us -> 4.05 us  [the longest x2 2.03 us: blocked(): blocks = [own] + [lax.ppermute(own, both, way) for way in (ahead, back)]]
    all_to_all x3, blocking collectives: 41.3 us -> 40.2 us  [swap(): return lax.all_to_all(v, axis, split_axis=0, concat_axis=0, tiled=True)]
    rev x0 -> x1, local copies, waits for them, and re-layouts: none -> 0.77 us  [blocked(): fixed[::-1]]
  transfers between devices with their start and end apart: 2 -> 4, of which waited for: 1 -> 1; matrix products, arithmetic and copies ran while one was open for 0% -> 1% of each run, Pallas kernels for 0% -> 0%
where the time goes in v5:
time: 54.5 us; the launch traced here: 54.2 us
  blocking collectives  40.2 us (74%)
  Pallas kernels  7.19 us (13%)
  starting transfers between devices  4.05 us (7%)
  waiting for transfers between devices  1.97 us (4%)
  local copies, waits for them, and re-layouts  0.77 us (1%)
    all_to_all x3, blocking collectives, swap(): return lax.all_to_all(v, axis, split_axis=0, concat_axis=0, tiled=True)  40.2 us
    pallas_call x1, Pallas kernels, blocked(): call(functools.partial(iterations_kernel, orders), [(images * groups, 2 *...  4.11 us
    ppermute x2, starting transfers between devices, blocked(): blocks = [own] + [lax.ppermute(own, both, way) for way in (ahead, back)]  2.03 us
    ppermute x2, starting transfers between devices, blocked(): lax.ppermute(fixed, both, way)  2.03 us
    ppermute x2, waiting for transfers between devices, blocked(): lax.ppermute(fixed, both, way)  1.97 us
    pallas_call x1, Pallas kernels, blocked(): call(functools.partial(pack_kernel, orders), [(groups, 2 * images) + tile...  1.83 us
  transfers between devices with their start and end apart: 4, of which 1 were waited for; matrix products, arithmetic and copies ran while one was open for 1% of the time, Pallas kernels for 0%

profile of v5, /device:TPU:0, one launch (start us, length us, event | category | flops | bytes accessed | tf_op | source)
XLA Modules:
  0.0 54.2 jit_solution(11444208011066050024)
XLA Ops:
  0.0 1.8 %shard_map.55 = (f32[8,8,8,128]{3,2,1,0:T(8,128)}, f32[6,8,128]{2,1,0:T(8,128)}) custom-call(f32[4,4,32,128]{3,2,1,0:T(8,128)} %path_ref.1, f32[4,32,128]{2,1,0:T(8,128)} %start_ref.1, f32[4,32,128]{2,1,0:T(8,128)} %end_ref.1, s32[4,32,128]{2,1,0:T(8,128)} %labels_ref.1, f32[4]{0:T(128)} %table_ref.1), custom_call_target="tpu_custom_call" | custom-call | tf_op jit(solution)/shard_map/pallas_call | solution.py:478
  1.8 16.2 %all_to_all.21.own_ref = f32[8,8,8,128]{3,2,1,0:T(8,128)S(1)} all-to-all(f32[8,8,8,128]{3,2,1,0:T(8,128)} %get-tuple-element.9), channel_id=1, replica_groups=mesh['img'=8,'gy'=4] {'img'}, dimensions={0} | all-to-all | bytes 524288 | tf_op jit(solution)/shard_map/all_to_all | solution.py:476
  18.1 0.0 collective-permute-start.1
  18.1 2.0 %collective-permute-start = (f32[8,8,8,128]{3,2,1,0:T(8,128)S(1)}, f32[8,8,8,128]{3,2,1,0:T(8,128)S(1)}, u32[]{:S(2)}, u32[]{:S(2)}) collective-permute-start(f32[8,8,8,128]{3,2,1,0:T(8,128)S(1)} %all_to_all.21.own_ref), channel_id=1, source_target_pairs={{3,0},{0,4},{4,12},{12,8},{8,16},{16,20},{20,28},{28,24},{24,25},{... | collective-permute-start | bytes 786440 | tf_op jit(solution)/shard_map/ppermute | solution.py:486
  20.1 0.0 collective-permute-start.3
  20.1 2.0 %collective-permute-start.2 = (f32[6,8,128]{2,1,0:T(8,128)}, f32[6,8,128]{2,1,0:T(8,128)S(1)}, u32[]{:S(2)}, u32[]{:S(2)}) collective-permute-start(f32[6,8,128]{2,1,0:T(8,128)} %get-tuple-element.10), channel_id=1, source_target_pairs={{3,0},{0,4},{4,12},{12,8},{8,16},{16,20},{20,28},{28,24},{24,25},{... | collective-permute-start | bytes 73736 | tf_op jit(solution)/shard_map/ppermute | solution.py:487
  22.1 0.8 %rev.3.fixed_ref = f32[6,8,128]{2,1,0:T(8,128)S(1)} reverse(f32[6,8,128]{2,1,0:T(8,128)} %get-tuple-element.10), dimensions={0} | reverse | bytes 49152 | tf_op jit(solution)/shard_map/rev | solution.py:487
  22.9 2.0 %collective-permute-done.3.fixed_next_ref = f32[6,8,128]{2,1,0:T(8,128)S(1)} collective-permute-done((f32[6,8,128]{2,1,0:T(8,128)}, f32[6,8,128]{2,1,0:T(8,128)S(1)}, u32[]{:S(2)}, u32[]{:S(2)}) %collective-permute-start.3) | collective-permute-done | bytes 24608 | tf_op jit(solution)/shard_map/ppermute | solution.py:487
  24.9 0.0 collective-permute-done.2.fixed_prev_ref
  24.9 0.0 collective-permute-done.1.next_ref
  24.9 0.0 collective-permute-done.prev_ref
  24.9 4.1 %shard_map.56 = (f32[32,12,8,128]{3,2,1,0:T(8,128)S(1)}, f32[32,128]{1,0:T(8,128)S(1)}) custom-call(f32[8,8,8,128]{3,2,1,0:T(8,128)S(1)} %all_to_all.21.own_ref, f32[8,8,8,128]{3,2,1,0:T(8,128)S(1)} %collective-permute-done.prev_ref, f32[8,8,8,128]{3,2,1,0:T(8,128)S(1)} %collective-permute-done.1.next_ref, f32[6,8,128]{2,1,0:T(8,128)S(1)} %rev.3.fixed_ref, ...), custom_call_target="tpu_custom_call" | custom-call | tf_op jit(solution)/shard_map/pallas_call | solution.py:488
  29.0 12.3 %all_to_all.22 = f32[32,1,128]{2,1,0:T(1,128)S(1)} all-to-all(f32[32,1,128]{2,1,0:T(1,128)S(1)} %bitcast.4), channel_id=1, replica_groups=mesh['img'=8,'gy'=4] {'img','gy'}, dimensions={0} | all-to-all | bytes 32768 | tf_op jit(solution)/shard_map/all_to_all | solution.py:476
  41.3 0.5 shard_map.57
  41.7 11.6 %all_to_all.23.data_ref = f32[8,8,8,128]{3,2,1,0:T(8,128)S(1)} all-to-all(f32[8,8,8,128]{3,2,1,0:T(8,128)S(1)} %shard_map.57), channel_id=1, replica_groups=mesh['img'=8,'gy'=4] {'img'}, dimensions={0} | all-to-all | bytes 524288 | tf_op jit(solution)/shard_map/all_to_all | solution.py:476
  53.4 0.8 %shard_map.58 = f32[4,4,32,128]{3,2,1,0:T(8,128)} custom-call(f32[8,8,8,128]{3,2,1,0:T(8,128)S(1)} %all_to_all.23.data_ref), custom_call_target="tpu_custom_call" | custom-call | tf_op jit(solution)/shard_map/pallas_call | solution.py:503
Async XLA Ops:
  18.1 6.8 %collective-permute-start.1 = (f32[8,8,8,128]{3,2,1,0:T(8,128)S(1)}, f32[8,8,8,128]{3,2,1,0:T(8,128)S(1)}, u32[]{:S(2)}, u32[]{:S(2)}) collective-permute-start(f32[8,8,8,128]{3,2,1,0:T(8,128)S(1)} %all_to_all.21.own_ref), channel_id=1, source_target_pairs={{0,3},{4,0},{12,4},{8,12},{16,8},{20,16},{28,20},{24,28},{25,24},{... | collective-permute-start | bytes 786440 | tf_op jit(solution)/shard_map/ppermute | solution.py:486
  18.1 6.8 %collective-permute-start = (f32[8,8,8,128]{3,2,1,0:T(8,128)S(1)}, f32[8,8,8,128]{3,2,1,0:T(8,128)S(1)}, u32[]{:S(2)}, u32[]{:S(2)}) collective-permute-start(f32[8,8,8,128]{3,2,1,0:T(8,128)S(1)} %all_to_all.21.own_ref), channel_id=1, source_target_pairs={{3,0},{0,4},{4,12},{12,8},{8,16},{16,20},{20,28},{28,24},{24,25},{... | collective-permute-start | bytes 786440 | tf_op jit(solution)/shard_map/ppermute | solution.py:486
  20.1 4.8 %collective-permute-start.3 = (f32[6,8,128]{2,1,0:T(8,128)}, f32[6,8,128]{2,1,0:T(8,128)S(1)}, u32[]{:S(2)}, u32[]{:S(2)}) collective-permute-start(f32[6,8,128]{2,1,0:T(8,128)} %get-tuple-element.10), channel_id=1, source_target_pairs={{0,3},{4,0},{12,4},{8,12},{16,8},{20,16},{28,20},{24,28},{25,24},{... | collective-permute-start | bytes 73736 | tf_op jit(solution)/shard_map/ppermute | solution.py:487
  20.1 4.8 %collective-permute-start.2 = (f32[6,8,128]{2,1,0:T(8,128)}, f32[6,8,128]{2,1,0:T(8,128)S(1)}, u32[]{:S(2)}, u32[]{:S(2)}) collective-permute-start(f32[6,8,128]{2,1,0:T(8,128)} %get-tuple-element.10), channel_id=1, source_target_pairs={{3,0},{0,4},{4,12},{12,8},{8,16},{16,20},{20,28},{28,24},{24,25},{... | collective-permute-start | bytes 73736 | tf_op jit(solution)/shard_map/ppermute | solution.py:487
